TPU v7x, 128 devices: a whole 4x4x4 slice. The times are simulated.
128 devices in a mesh: lat: 8 (over x, z_hi), lon: 16 (over z_lo, y, core).
Axes of the slice: x: 4, y: 4, z: 4 (z_hi: 2, z_lo: 2; z = z_hi * 2 + z_lo), core: 2. Of those that a mesh axis runs over, the one named last changes fastest.
Arguments:
- fine_field: bfloat16 [4, 96, 192, 512], P(None, 'lat', 'lon'), may hold values from -6 to 6
- offsets: int32 [4], replicated, may hold values from 1 to 11, as said below
- fine_prenorm: float32 [512], replicated, may hold values from 0.25 to 1.75
- fine_triple: bfloat16 [512, 1536], replicated, may hold values from -0.25 to 0.25
- fine_bias: float32 [16, 144, 144], replicated, may hold values from -160 to 160
- fine_output: bfloat16 [512, 512], replicated, may hold values from -0.25 to 0.25
- fine_midnorm: float32 [512], replicated, may hold values from 0.25 to 1.75
- fine_expand: bfloat16 [512, 2048], replicated, may hold values from -0.25 to 0.25
- fine_reduce: bfloat16 [2048, 512], replicated, may hold values from -0.125 to 0.125
- merge_gain: float32 [2048], replicated, may hold values from 0.25 to 1.75
- merge_weight: bfloat16 [2048, 1024], replicated, may hold values from -0.125 to 0.125
- coarse_prenorm: float32 [1024], replicated, may hold values from 0.25 to 1.75
- coarse_triple: bfloat16 [1024, 3072], P(None, 'lon'), may hold values from -0.1875 to 0.1875
- coarse_bias: float32 [32, 144, 144], P('lon'), may hold values from -160 to 160
- coarse_output: bfloat16 [1024, 1024], P('lon'), may hold values from -0.1875 to 0.1875
- coarse_midnorm: float32 [1024], replicated, may hold values from 0.25 to 1.75
- coarse_expand: bfloat16 [1024, 4096], P(None, 'lon'), may hold values from -0.1875 to 0.1875
- coarse_reduce: bfloat16 [4096, 1024], P('lon'), may hold values from -0.09375 to 0.09375
- upsample_weight: bfloat16 [1024, 2048], replicated, may hold values from -0.1875 to 0.1875
Outputs:
- blended: bfloat16 [4, 96, 192, 512], P(None, 'lat', 'lon')
- coarse_state: bfloat16 [4, 48, 96, 1024], P(None, 'lat', 'lon')
Inputs may be any that keep to these rules, and one draw needn't show every extreme that they name: `offsets`: entries 0 and 2 lie in 1 to 5, entries 1 and 3 in 1 to 11; in every draw entry 0 or entry 2 equals 5, and entry 1 or entry 3 equals 11.
All inputs are finite; a program needn't handle non-finite values.
Results may differ from a plain program's by a relative error of at most 0.024.
Values may be sent and summed in bfloat16 or wider, within the bound.
No kernel may reach another device: no remote copies, remote signals or barrier semaphores. Data moves between devices by JAX's collectives and lax.ppermute only.
A program may use at most 128 MiB of HBM per device.

v0:
```python
import jax
import jax.numpy as jnp
from jax import lax
from jax.sharding import PartitionSpec as P
from jax.experimental import pallas as pl
from jax.experimental.pallas import tpu as pltpu

BF = jnp.bfloat16
F32 = jnp.float32
EPS = 1e-05
NEG = -1e30
WT = 144
VLIM = 56 * 1024 * 1024


def full_spec(n, smem=()):
    return [
        pl.BlockSpec(memory_space=pltpu.SMEM) if i in smem else pl.BlockSpec(memory_space=pltpu.VMEM)
        for i in range(n)
    ]


def norm_rows(x, gain):
    mean = jnp.mean(x, axis=-1, keepdims=True)
    off = x - mean
    var = jnp.mean(off * off, axis=-1, keepdims=True)
    return off * lax.rsqrt(var + EPS) * gain


def dot_nt(a, b):
    return lax.dot_general(a, b, (((1,), (1,)), ((), ())), preferred_element_type=F32)


def dot_nn(a, b):
    return jnp.dot(a, b, preferred_element_type=F32)


def rows_to_tiles(rows, tiles, first):
    count = rows.shape[0]
    for c in range(8):
        tiles[pl.ds(first * 8 + c, count, stride=8), :] = rows[:, 128 * c : 128 * c + 128]


def tiles_to_rows(tiles, first, count):
    return [tiles[pl.ds(first * 8 + c, count, stride=8), :] for c in range(8)]


def attend_group(q, k, v, bias_of, extra, scale, store):
    lane_head = lax.broadcasted_iota(jnp.int32, (WT, 128), 1) // 32
    total = None
    for h in range(4):
        pick = lane_head == h
        qh = jnp.where(pick, q, jnp.zeros_like(q))
        vh = jnp.where(pick, v, jnp.zeros_like(v))
        s = dot_nt(qh, k) * scale + (bias_of(h) + extra)
        top = jnp.max(s, axis=-1, keepdims=True)
        p = jnp.exp(s - top)
        inv = 1.0 / jnp.sum(p, axis=-1, keepdims=True)
        o = dot_nn(p.astype(BF), vh) * inv
        total = o if total is None else total + o
    store(total)


def region_mask(thr):
    def reg(dim):
        t = lax.broadcasted_iota(jnp.int32, (WT, WT), dim)
        return jnp.where(t >= 72, t - 72, t) >= thr

    return jnp.where(reg(0) == reg(1), 0.0, NEG).astype(F32)


def fine_attn_kernel(sc_ref, own_ref, lon_ref, lat_ref, gain_ref, w_ref, bias_ref, out_ref, ext, xw, q_s, k_s, v_s, mask_s, o_s):
    s0 = sc_ref[0]
    s1 = sc_ref[1]
    for l in range(4):
        for r in range(12):
            ext[l, r, 0:12] = own_ref[l, r].astype(F32)
            ext[l, r, 12:23] = lon_ref[l, r].astype(F32)
        for r in range(5):
            ext[l, 12 + r, 0:23] = lat_ref[l, r].astype(F32)
    for dp in range(2):
        for lr in range(2):
            for a in range(2):
                for b in range(6):
                    row = ((dp * 2 + lr) * 12 + a * 6 + b) * 12
                    full = ext[dp * 2 + a, s0 + lr * 6 + b]
                    xw[row : row + 12] = pltpu.roll(full, 24 - s1, 0)[0:12]
    gain = gain_ref[...]

    def project(i, _):
        rows = pl.ds(i * WT, WT)
        xn = norm_rows(xw[rows], gain).astype(BF)
        q_s[rows] = dot_nn(xn, w_ref[0]).astype(BF)
        k_s[rows] = dot_nn(xn, w_ref[1]).astype(BF)
        v_s[rows] = dot_nn(xn, w_ref[2]).astype(BF)
        return 0

    lax.fori_loop(0, 4, project, 0)

    def window(i, _):
        thr = jnp.where(i % 2 == 1, sc_ref[2], 1000)
        mask_s[...] = region_mask(thr)
        rows = pl.ds(i * WT, WT)
        for j in range(4):
            cols = slice(128 * j, 128 * j + 128)

            def store(total, cols=cols):
                o_s[rows, cols] = total

            attend_group(
                q_s[rows, cols], k_s[rows, cols], v_s[rows, cols],
                lambda h, j=j: bias_ref[4 * j + h], mask_s[...], 32 ** (-0.5), store,
            )
        return 0

    lax.fori_loop(0, 4, window, 0)
    for dp in range(2):
        for lr in range(2):
            for a in range(2):
                for b in range(6):
                    row = ((dp * 2 + lr) * 12 + a * 6 + b) * 12
                    out_ref[dp * 2 + a, lr * 6 + b] = o_s[row : row + 12].astype(BF)


def fine_attention(scalars, own, lon, lat, gain, weights, bias):
    return pl.pallas_call(
        fine_attn_kernel,
        out_shape=jax.ShapeDtypeStruct((4, 12, 12, 512), BF),
        in_specs=full_spec(7, (0,)),
        out_specs=pl.BlockSpec(memory_space=pltpu.VMEM),
        scratch_shapes=[
            pltpu.VMEM((4, 17, 24, 512), F32),
            pltpu.VMEM((576, 512), F32),
            pltpu.VMEM((576, 512), BF),
            pltpu.VMEM((576, 512), BF),
            pltpu.VMEM((576, 512), BF),
            pltpu.VMEM((WT, WT), F32),
            pltpu.VMEM((576, 512), F32),
        ],
        compiler_params=pltpu.CompilerParams(vmem_limit_bytes=VLIM),
        name="fine_attention",
    )(scalars, own, lon, lat, gain, weights, bias)


def fine_post_kernel(sc_ref, own_ref, lon_ref, lat_ref, x_ref, wo_ref, g_ref, we_ref, wr_ref, mg_ref, wm_ref, fs_ref, ci_ref, ext, xf, mf, xp, mp, tiles):
    r0 = 5 - sc_ref[0]
    turn = 16 + sc_ref[1]
    for l in range(4):
        for r in range(12):
            ext[l, 5 + r, 16:28] = own_ref[l, r].astype(F32)
            ext[l, 5 + r, 5:16] = lon_ref[l, r].astype(F32)
            own_x = x_ref[l, r].astype(F32)
            for c in range(4):
                xf[c, l, r, 0:12] = own_x[:, 128 * c : 128 * c + 128]
        for r in range(5):
            ext[l, r, 5:28] = lat_ref[l, r].astype(F32)
    for l in range(4):
        for r in range(12):
            turned = pltpu.roll(ext[l, r0 + r], turn, 0)[0:16]
            for c in range(4):
                mf[c, l, r] = turned[:, 128 * c : 128 * c + 128]
    for b in range(2):
        for a in range(2):
            for p in range(4):
                for i in range(6):
                    row = (2 * b + a) * WT + p * 36 + i * 6
                    for c in range(4):
                        cs = slice(128 * c, 128 * c + 128)
                        mp[row : row + 6, cs] = mf[c, p, 2 * i + a, pl.ds(b, 6, stride=2), :]
                        xp[row : row + 6, cs] = xf[c, p, 2 * i + a, pl.ds(b, 6, stride=2), :]
    gain = g_ref[...]
    def block(i, _):
        rows = pl.ds(i * WT, WT)
        att = (xp[rows] + dot_nn(mp[rows].astype(BF), wo_ref[...])).astype(BF).astype(F32)
        xn = norm_rows(att, gain).astype(BF)
        hid = jax.nn.gelu(dot_nn(xn, we_ref[...])).astype(BF)
        fs_ref[i] = (att + dot_nn(hid, wr_ref[...])).astype(BF)
        return 0

    lax.fori_loop(0, 4, block, 0)
    parts = [fs_ref[i].astype(F32) for i in range(4)]
    mean = sum(jnp.sum(v, axis=-1, keepdims=True) for v in parts) * (1.0 / 2048)
    parts = [v - mean for v in parts]
    var = sum(jnp.sum(v * v, axis=-1, keepdims=True) for v in parts) * (1.0 / 2048)
    inv = lax.rsqrt(var + EPS)
    acc = None
    for i in range(4):
        cs = slice(512 * i, 512 * i + 512)
        t = dot_nn((parts[i] * inv * mg_ref[:, cs]).astype(BF), wm_ref[cs, :])
        acc = t if acc is None else acc + t
    rows_to_tiles(acc, tiles, 0)
    ci_ref[...] = tiles[...].reshape(4, 6, 6, 8, 128).astype(BF)


def fine_post(scalars, own, lon, lat, field, wo, gain, we, wr, mg, wm):
    return pl.pallas_call(
        fine_post_kernel,
        out_shape=(jax.ShapeDtypeStruct((4, WT, 512), BF), jax.ShapeDtypeStruct((4, 6, 6, 8, 128), BF)),
        in_specs=full_spec(11, (0,)),
        out_specs=(pl.BlockSpec(memory_space=pltpu.VMEM), pl.BlockSpec(memory_space=pltpu.VMEM)),
        scratch_shapes=[
            pltpu.VMEM((4, 17, 32, 512), F32),
            pltpu.VMEM((4, 4, 12, 16, 128), F32),
            pltpu.VMEM((4, 4, 12, 16, 128), F32),
            pltpu.VMEM((576, 512), F32),
            pltpu.VMEM((576, 512), F32),
            pltpu.VMEM((WT * 8, 128), F32),
        ],
        compiler_params=pltpu.CompilerParams(vmem_limit_bytes=VLIM),
        name="fine_post",
    )(scalars, own, lon, lat, field, wo, gain, we, wr, mg, wm)


def coarse_attn_kernel(sc_ref, own_ref, next_ref, gain_ref, g_ref, out_ref, ext, tiles, xf, xn, acc, mask_s):
    j = pl.program_id(0)

    @pl.when(j == 0)
    def _():
        s3 = sc_ref[3]
        for half in range(2):
            for a in range(2):
                ext[a, :, 6 * half : 6 * half + 6] = own_ref[half, a].astype(F32)
                ext[a, :, 12 + 6 * half : 18 + 6 * half] = next_ref[half, a].astype(F32)
        for a in range(2):
            for b in range(6):
                row = (a * 6 + b) * 96
                tiles[row : row + 96] = ext[a, b, pl.ds(s3, 12)].reshape(96, 128)
        for c, part in enumerate(tiles_to_rows(tiles, 0, WT)):
            xf[:, 128 * c : 128 * c + 128] = part
        xn[...] = norm_rows(xf[...], gain_ref[...]).astype(BF)
        acc[...] = xf[...]
        mask_s[...] = region_mask(sc_ref[4])

    def rows_of(first, count):
        return jnp.concatenate([g_ref[0, first : first + count], g_ref[1, first : first + count]], axis=0)

    x = xn[...]
    q = dot_nt(x, rows_of(0, 64)).astype(BF)
    k = dot_nt(x, rows_of(64, 64)).astype(BF)
    v = dot_nt(x, rows_of(128, 64)).astype(BF)

    def bias_of(h):
        first = (h % 2) * 512
        hi = g_ref[h // 2, 256:400, first : first + WT].astype(F32)
        return hi + g_ref[h // 2, 256:400, first + 256 : first + 256 + WT].astype(F32)

    def store(total):
        acc[...] += dot_nn(total.astype(BF), rows_of(192, 64))

    attend_group(q, k, v, bias_of, mask_s[...], 32 ** (-0.5), store)

    @pl.when(j == 7)
    def _():
        rows_to_tiles(acc[...], tiles, 0)
        out_ref[...] = tiles[...].reshape(2, 6, 12, 8, 128).astype(BF)


def coarse_attention(scalars, own, ahead, gain, packed):
    vm = lambda: pl.BlockSpec(memory_space=pltpu.VMEM)
    return pl.pallas_call(
        coarse_attn_kernel,
        grid=(8,),
        out_shape=jax.ShapeDtypeStruct((2, 6, 12, 8, 128), BF),
        in_specs=[
            pl.BlockSpec(memory_space=pltpu.SMEM), vm(), vm(), vm(),
            pl.BlockSpec((2, 400, 1024), lambda j: (j, 0, 0)),
        ],
        out_specs=vm(),
        scratch_shapes=[
            pltpu.VMEM((2, 6, 24, 8, 128), F32),
            pltpu.VMEM((WT * 8, 128), F32),
            pltpu.VMEM((WT, 1024), F32),
            pltpu.VMEM((WT, 1024), BF),
            pltpu.VMEM((WT, 1024), F32),
            pltpu.VMEM((WT, WT), F32),
        ],
        compiler_params=pltpu.CompilerParams(vmem_limit_bytes=VLIM, dimension_semantics=("arbitrary",)),
        name="coarse_attention",
    )(scalars, own, ahead, gain, packed)


def coarse_ff_kernel(own_ref, across_ref, mate_ref, gain_ref, g_ref, keep_ref, send_ref, tiles, xn, acc):
    j = pl.program_id(0)

    @pl.when(j == 0)
    def _():
        sources = (own_ref[...], across_ref[...], mate_ref[0], mate_ref[1])
        for i, block in enumerate(sources):
            tiles[...] = block.astype(F32).reshape(WT * 8, 128)
            x = jnp.concatenate(tiles_to_rows(tiles, 0, WT), axis=1)
            xn[WT * i : WT * i + WT] = norm_rows(x, gain_ref[...]).astype(BF)
        acc[...] = jnp.zeros_like(acc)

    hid = jax.nn.gelu(dot_nt(xn[...], g_ref[0, 0:256])).astype(BF)
    acc[...] += dot_nn(hid, g_ref[0, 256:512])

    @pl.when(j == 3)
    def _():
        keep_ref[...] = acc[0 : 2 * WT]
        send_ref[...] = acc[2 * WT : 4 * WT].astype(BF)


def coarse_ff(own, across, mate, gain, packed):
    vm = lambda: pl.BlockSpec(memory_space=pltpu.VMEM)
    return pl.pallas_call(
        coarse_ff_kernel,
        grid=(4,),
        out_shape=(jax.ShapeDtypeStruct((2 * WT, 1024), F32), jax.ShapeDtypeStruct((2 * WT, 1024), BF)),
        in_specs=[vm(), vm(), vm(), vm(), pl.BlockSpec((1, 512, 1024), lambda j: (j, 0, 0))],
        out_specs=(vm(), vm()),
        scratch_shapes=[
            pltpu.VMEM((WT * 8, 128), F32),
            pltpu.VMEM((4 * WT, 1024), BF),
            pltpu.VMEM((4 * WT, 1024), F32),
        ],
        compiler_params=pltpu.CompilerParams(vmem_limit_bytes=VLIM, dimension_semantics=("arbitrary",)),
        name="coarse_ff",
    )(own, across, mate, gain, packed)


def blend_kernel(mid_ref, keep_ref, mate_ref, across_ref, wu_ref, fs_ref, out_ref, cs_ref, tiles, rows_s, grid_s):
    tiles[...] = mid_ref[...].astype(F32).reshape(WT * 8, 128)
    mid = jnp.concatenate(tiles_to_rows(tiles, 0, WT), axis=1)
    added = keep_ref[0:WT] + mate_ref[0:WT].astype(F32) + across_ref[...].astype(F32)
    rows_s[...] = mid + added
    state = rows_s[...].astype(BF)
    for p in range(4):
        for i in range(6):
            row = p * 36 + i * 6
            cs_ref[p, i] = rows_s[row : row + 6].astype(BF)
    for blk in range(4):
        b, a = blk // 2, blk % 2
        e = dot_nn(state, wu_ref[:, 512 * blk : 512 * blk + 512])
        t = fs_ref[blk].astype(F32) + e
        for p in range(4):
            for i in range(6):
                row = p * 36 + i * 6
                for c in range(4):
                    cs = slice(128 * c, 128 * c + 128)
                    grid_s[c, p, 2 * i + a, pl.ds(b, 6, stride=2), :] = t[row : row + 6, cs]
    for p in range(4):
        for r in range(12):
            for c in range(4):
                out_ref[p, r, :, 128 * c : 128 * c + 128] = grid_s[c, p, r, 0:12].astype(BF)


def blend(mid, keep, mate, across, wu, fs):
    return pl.pallas_call(
        blend_kernel,
        out_shape=(jax.ShapeDtypeStruct((4, 12, 12, 512), BF), jax.ShapeDtypeStruct((4, 6, 6, 1024), BF)),
        in_specs=full_spec(6),
        out_specs=(pl.BlockSpec(memory_space=pltpu.VMEM), pl.BlockSpec(memory_space=pltpu.VMEM)),
        scratch_shapes=[
            pltpu.VMEM((WT * 8, 128), F32),
            pltpu.VMEM((WT, 1024), F32),
            pltpu.VMEM((4, 4, 12, 16, 128), F32),
        ],
        compiler_params=pltpu.CompilerParams(vmem_limit_bytes=VLIM),
        name="blend",
    )(mid, keep, mate, across, wu, fs)


WL = 6
WW = 12


def shifted(block, axis, distance):
    devices = range(lax.axis_size(axis))
    route = [((i - distance) % len(devices), i) for i in devices]
    return lax.ppermute(block, axis, route)


def swapped(block, bit):
    return lax.ppermute(block, "lon", [(i, i ^ bit) for i in range(lax.axis_size("lon"))])


def chip_shifted(block, distance):
    count = lax.axis_size("lon")
    return lax.ppermute(block, "lon", [((i - 2 * distance) % count, i) for i in range(count)])


def in_order(core, mine, other):
    first = jnp.where(core == 0, mine, other)
    second = jnp.where(core == 0, other, mine)
    return jnp.stack([first, second])


def pack_attention(triple, output, bias):
    wide = triple.shape[0]
    columns = triple.reshape(wide, 2, 3, 32).transpose(2, 1, 3, 0).reshape(192, wide)
    padded = jnp.pad(bias, ((0, 0), (0, 0), (0, 256 - WT)))
    high = lax.reduce_precision(padded, 8, 7)
    low = padded - high
    both = jnp.stack([high, low], axis=1).astype(BF).transpose(2, 0, 1, 3).reshape(WT, 1024)
    return jnp.concatenate([columns, output, both], axis=0)


def body(
    fine_field,
    offsets,
    fine_prenorm,
    fine_triple,
    fine_bias,
    fine_output,
    fine_midnorm,
    fine_expand,
    fine_reduce,
    merge_gain,
    merge_weight,
    coarse_prenorm,
    coarse_triple,
    coarse_bias,
    coarse_output,
    coarse_midnorm,
    coarse_expand,
    coarse_reduce,
    upsample_weight,
):
    levels, lat_rows, lon_cols, channels = fine_field.shape
    lat_count = lax.axis_size("lat")
    lat_index = lax.axis_index("lat")
    fine_lat = offsets[0]
    fine_lon = offsets[1]
    coarse_lat = offsets[2]
    coarse_lon = offsets[3]
    core = lax.axis_index("lon") % 2
    attn_pack = pack_attention(coarse_triple, coarse_output, coarse_bias)
    attn_all = lax.all_gather(attn_pack, "lon", axis=0, tiled=False)
    ff_pack = jnp.concatenate([coarse_expand.T, coarse_reduce], axis=0)
    rings = [[z * 8 + y * 2 + c for y in range(4)] for z in range(2) for c in range(2)]
    ff_all = lax.all_gather(ff_pack, "lon", axis=0, tiled=False, axis_index_groups=rings)
    lon_ahead = shifted(fine_field[:, :, : WW - 1], "lon", -1)
    lat_ahead = shifted(
        jnp.concatenate([fine_field[:, : WL - 1], lon_ahead[:, : WL - 1]], axis=2), "lat", -1
    )
    half_rows = lat_rows // 2
    half_cols = lon_cols // 2
    last_band = lat_index == lat_count - 1
    scalars = jnp.stack(
        [
            fine_lat,
            fine_lon,
            jnp.where(last_band, 12 * (WL - fine_lat), 1000),
            coarse_lon,
            jnp.where(last_band, 12 * (WL - coarse_lat), 1000),
        ]
    )
    triple_heads = fine_triple.reshape(channels, -1, 3, 32).transpose(2, 0, 1, 3)
    triple_heads = triple_heads.reshape(3, channels, channels)
    mixed_fine = fine_attention(
        scalars, fine_field, lon_ahead, lat_ahead, fine_prenorm[None], triple_heads, fine_bias
    )
    lon_behind = shifted(mixed_fine[:, :, lon_cols - WW + 1 :], "lon", 1)
    tail = lat_rows - WL + 1
    lat_behind = shifted(
        jnp.concatenate([lon_behind[:, tail:], mixed_fine[:, tail:]], axis=2), "lat", 1
    )
    fine_state, coarse_own = fine_post(
        scalars, mixed_fine, lon_behind, lat_behind, fine_field, fine_output, fine_midnorm[None],
        fine_expand, fine_reduce, merge_gain[None], merge_weight,
    )
    rows_ahead = shifted(coarse_own[:, : WL - 1], "lat", -1)
    framed = lax.dynamic_slice_in_dim(
        jnp.concatenate([coarse_own, rows_ahead], axis=1), coarse_lat, half_rows, axis=1
    )
    mine = lax.dynamic_slice_in_dim(framed, 2 * core, 2, axis=0)
    other = swapped(lax.dynamic_slice_in_dim(framed, 2 - 2 * core, 2, axis=0), 1)
    chip = in_order(core, mine, other)
    chip_ahead = chip_shifted(chip, -1)
    mid_framed = coarse_attention(scalars, chip, chip_ahead, coarse_prenorm[None], attn_all)
    cols_behind = chip_shifted(mid_framed[:, :, 1:], 1)
    spread = jnp.concatenate([cols_behind, mid_framed], axis=2)
    first = WW - 1 - coarse_lon
    mine = lax.dynamic_slice_in_dim(spread, first + half_cols * core, half_cols, axis=2)
    other = swapped(
        lax.dynamic_slice_in_dim(spread, first + half_cols * (1 - core), half_cols, axis=2), 1
    )
    levels_all = in_order(core, mine, other).reshape(levels, half_rows, half_cols, 8, 128)
    rows_behind = shifted(levels_all[:, 1:], "lat", 1)
    mid_own = lax.dynamic_slice_in_dim(
        jnp.concatenate([rows_behind, levels_all], axis=1), WL - 1 - coarse_lat, half_rows, axis=1
    )
    mid_own = mid_own.reshape(WT, 8, 128)
    across = swapped(mid_own, 8)
    mate = swapped(jnp.stack([mid_own, across]), 1)
    keep, send = coarse_ff(mid_own, across, mate, coarse_midnorm[None], ff_all)
    from_mate = swapped(send, 1)
    from_across = swapped((keep[WT:] + from_mate[WT:].astype(F32)).astype(BF), 8)
    return blend(mid_own, keep, from_mate, from_across, upsample_weight, fine_state)


def solution(mesh):
    placed = (
        P(None, "lat", "lon", None),
        P(),
        P(),
        P(),
        P(),
        P(),
        P(),
        P(),
        P(),
        P(),
        P(),
        P(),
        P(None, "lon"),
        P("lon", None, None),
        P("lon", None),
        P(),
        P(None, "lon"),
        P("lon", None),
        P(),
    )
    return jax.shard_map(
        body,
        mesh=mesh,
        in_specs=placed,
        out_specs=(P(None, "lat", "lon", None), P(None, "lat", "lon", None)),
        check_vma=False,
    )
```

profile of v0, /device:TPU:1, one launch (start us, length us, event | category | flops | bytes accessed | tf_op | source)
XLA Modules:
  0.0 236.0 jit_solution(13972953852247500881)
XLA Ops:
  7.2 1.0 fusion.3
  8.3 0.3 copy.54
  8.6 0.2 reshape.35
  8.9 0.9 pad_maximum_fusion.1
  9.9 0.2 copy.55
  10.2 0.2 copy-done.11
  10.3 1.0 pad_maximum_fusion
  11.4 0.2 slice.50
  11.6 1.5 collective-permute-start
  13.1 0.1 copy.46.own_ref.x_ref
  13.3 8.1 %collective-permute-done = bf16[4,12,11,512]{3,0,2,1:T(4,128)(2,1)S(1)} collective-permute-done((bf16[4,12,11,512]{3,0,2,1:T(4,128)(2,1)S(1)}, bf16[4,12,11,512]{3,0,2,1:T(4,128)(2,1)S(1)}, u32[]{:S(2)}, u32[]{:S(2)}) %collective-permute-start) | collective-permute-done | bytes 540704 | tf_op jit(solution)/shard_map/ppermute | solution.py:370
  21.4 0.1 copy.47.lon_ref
  21.6 1.0 pad_maximum_fusion.3
  22.6 5.8 %collective-permute-start.1 = (bf16[4,5,23,512]{3,2,1,0:T(8,128)(2,1)}, bf16[4,5,23,512]{3,2,1,0:T(8,128)(2,1)}, u32[]{:S(2)}, u32[]{:S(2)}) collective-permute-start(bf16[4,5,23,512]{3,2,1,0:T(8,128)(2,1)} %pad_maximum_fusion.3), channel_id=1, source_target_pairs={{16,0},{32,16},{48,32},{64,48},{80,64},{96,80},{112,96},{0,112},{1... | collective-permute-start | bytes 1413128 | tf_op jit(solution)/shard_map/ppermute | solution.py:370
  28.4 0.7 fusion.6
  30.4 0.7 copy.44
  31.1 0.2 copy.45
  31.3 1.6 copy.48.w_ref
  32.8 1.3 pad_add_fusion.sc_ref
  34.1 13.7 %collective-permute-done.1.lat_ref = bf16[4,5,23,512]{3,2,1,0:T(8,128)(2,1)} collective-permute-done((bf16[4,5,23,512]{3,2,1,0:T(8,128)(2,1)}, bf16[4,5,23,512]{3,2,1,0:T(8,128)(2,1)}, u32[]{:S(2)}, u32[]{:S(2)}) %collective-permute-start.1) | collective-permute-done | bytes 471072 | tf_op jit(solution)/shard_map/ppermute | solution.py:370
  47.8 12.4 %fine_attention.1.own_ref = bf16[4,12,12,512]{3,2,1,0:T(8,128)(2,1)} custom-call(s32[5]{0:T(128)} %pad_add_fusion.sc_ref, bf16[4,12,12,512]{3,2,1,0:T(8,128)(2,1)} %copy-done, bf16[4,12,11,512]{3,2,1,0:T(8,128)(2,1)} %copy-done.2, bf16[4,5,23,512]{3,2,1,0:T(8,128)(2,1)} %collective-permute-done.1.lat_ref, f32[1,512]{1,0:T(1,128)} %bitcast.58, ...), custom_call_target="tpu_custom_call" | custom-call | tf_op jit(solution)/shard_map/fine_attention/pallas_call | solution.py:126
  60.2 1.4 slice.63
  61.7 0.5 copy.49
  62.2 14.5 %collective-permute-done.2 = bf16[4,12,11,512]{3,0,2,1:T(4,128)(2,1)S(1)} collective-permute-done((bf16[4,12,11,512]{3,0,2,1:T(4,128)(2,1)S(1)}, bf16[4,12,11,512]{3,0,2,1:T(4,128)(2,1)S(1)}, u32[]{:S(2)}, u32[]{:S(2)}) %collective-permute-start.2) | collective-permute-done | bytes 540704 | tf_op jit(solution)/shard_map/ppermute | solution.py:370
  76.8 0.1 copy.51.lon_ref
  77.0 0.1 pad_maximum_fusion.4
  77.1 0.4 collective-permute-start.3
  77.5 21.3 %collective-permute-done.3.lat_ref = bf16[4,5,23,512]{3,2,1,0:T(8,128)(2,1)S(1)} collective-permute-done((bf16[4,5,23,512]{3,2,1,0:T(8,128)(2,1)S(1)}, bf16[4,5,23,512]{3,2,1,0:T(8,128)(2,1)S(1)}, u32[]{:S(2)}, u32[]{:S(2)}) %collective-permute-start.3) | collective-permute-done | bytes 471072 | tf_op jit(solution)/shard_map/ppermute | solution.py:370
  98.8 0.8 copy-done.12
  99.6 13.0 %fine_post.1 = (bf16[4,144,512]{2,1,0:T(8,128)(2,1)}, bf16[4,6,6,8,128]{4,3,2,1,0:T(8,128)(2,1)}) custom-call(s32[5]{0:T(128)} %pad_add_fusion.sc_ref, bf16[4,12,12,512]{3,2,1,0:T(8,128)(2,1)} %fine_attention.1.own_ref, bf16[4,12,11,512]{3,2,1,0:T(8,128)(2,1)} %copy-done.3, bf16[4,5,23,512]{3,2,1,0:T(8,128)(2,1)} %copy-done.12, ...), custom_call_target="tpu_custom_call" | custom-call | tf_op jit(solution)/shard_map/fine_post/pallas_call | solution.py:196
  112.6 1.0 slice.56
  113.6 5.6 %collective-permute-start.4 = (bf16[4,5,6,8,128]{4,3,2,1,0:T(8,128)(2,1)S(1)}, bf16[4,5,6,8,128]{4,3,2,1,0:T(8,128)(2,1)S(1)}, u32[]{:S(2)}, u32[]{:S(2)}) collective-permute-start(bf16[4,5,6,8,128]{4,3,2,1,0:T(8,128)(2,1)S(1)} %slice.56), channel_id=1, source_target_pairs={{16,0},{32,16},{48,32},{64,48},{80,64},{96,80},{112,96},{0,112},{1... | collective-permute-start | bytes 737288 | tf_op jit(solution)/shard_map/ppermute | solution.py:370
  121.1 1.0 constant_dynamic-update-slice_fusion.1
  122.1 2.5 %collective-permute-done.4 = bf16[4,5,6,8,128]{4,3,2,1,0:T(8,128)(2,1)S(1)} collective-permute-done((bf16[4,5,6,8,128]{4,3,2,1,0:T(8,128)(2,1)S(1)}, bf16[4,5,6,8,128]{4,3,2,1,0:T(8,128)(2,1)S(1)}, u32[]{:S(2)}, u32[]{:S(2)}) %collective-permute-start.4) | collective-permute-done | bytes 245792 | tf_op jit(solution)/shard_map/ppermute | solution.py:370
  124.7 1.0 collective-permute-start.5
  125.7 1.0 collective-permute-done.5
  126.8 3.7 %collective-permute-start.6 = (bf16[2,2,6,6,8,128]{5,4,3,2,1,0:T(8,128)(2,1)S(1)}, bf16[2,2,6,6,8,128]{5,4,3,2,1,0:T(8,128)(2,1)S(1)}, u32[]{:S(2)}, u32[]{:S(2)}) collective-permute-start(bf16[2,2,6,6,8,128]{5,4,3,2,1,0:T(8,128)(2,1)S(1)} %pad_maximum_fusion.5.own_ref), channel_id=1, source_target_pairs={{2,0},{3,1},{4,2},{5,3},{6,4},{7,5},{8,6},{9,7},{10,8},{11,9},{12,... | collective-permute-start | bytes 884744 | tf_op jit(solution)/shard_map/ppermute | solution.py:379
  130.5 12.8 %collective-permute-done.6.next_ref = bf16[2,2,6,6,8,128]{5,4,3,2,1,0:T(8,128)(2,1)S(1)} collective-permute-done((bf16[2,2,6,6,8,128]{5,4,3,2,1,0:T(8,128)(2,1)S(1)}, bf16[2,2,6,6,8,128]{5,4,3,2,1,0:T(8,128)(2,1)S(1)}, u32[]{:S(2)}, u32[]{:S(2)}) %collective-permute-start.6) | collective-permute-done | bytes 294944 | tf_op jit(solution)/shard_map/ppermute | solution.py:379
  143.3 0.7 copy-done.16
  144.0 13.3 %coarse_attention.1 = bf16[2,6,12,8,128]{4,3,2,1,0:T(8,128)(2,1)} custom-call(s32[5]{0:T(128)} %pad_add_fusion.sc_ref, bf16[2,2,6,6,8,128]{5,4,3,2,1,0:T(8,128)(2,1)} %copy-done.7, bf16[2,2,6,6,8,128]{5,4,3,2,1,0:T(8,128)(2,1)} %copy-done.16, f32[1,1024]{1,0:T(1,128)} %bitcast.56, bf16[16,400,1024]{2,1,0:T(8,128)(2,1)} %bitcast.40), custom_call_target="tpu_custom_call" | custom-call | tf_op jit(solution)/shard_map/coarse_attention/pallas_call | solution.py:260
  157.3 1.0 slice.66
  159.1 9.2 %collective-permute-done.7 = bf16[2,6,11,8,128]{4,3,2,1,0:T(8,128)(2,1)S(1)} collective-permute-done((bf16[2,6,11,8,128]{4,3,2,1,0:T(8,128)(2,1)S(1)}, bf16[2,6,11,8,128]{4,3,2,1,0:T(8,128)(2,1)S(1)}, u32[]{:S(2)}, u32[]{:S(2)}) %collective-permute-start.7) | collective-permute-done | bytes 270368 | tf_op jit(solution)/shard_map/ppermute | solution.py:379
  168.3 0.8 fusion.4
  169.1 2.1 collective-permute-start.8
  171.2 1.0 collective-permute-done.8
  172.2 1.1 select_bitcast_fusion.1
  173.4 3.1 %collective-permute-start.9 = (bf16[4,5,6,8,128]{4,3,2,1,0:T(8,128)(2,1)S(1)}, bf16[4,5,6,8,128]{4,3,2,1,0:T(8,128)(2,1)S(1)}, u32[]{:S(2)}, u32[]{:S(2)}) collective-permute-start(bf16[4,5,6,8,128]{4,3,2,1,0:T(8,128)(2,1)S(1)} %slice.67), channel_id=1, source_target_pairs={{112,0},{0,16},{16,32},{32,48},{48,64},{64,80},{80,96},{96,112},{1... | collective-permute-start | bytes 737288 | tf_op jit(solution)/shard_map/ppermute | solution.py:370
  177.7 8.4 %collective-permute-done.9 = bf16[4,5,6,8,128]{4,3,2,1,0:T(8,128)(2,1)S(1)} collective-permute-done((bf16[4,5,6,8,128]{4,3,2,1,0:T(8,128)(2,1)S(1)}, bf16[4,5,6,8,128]{4,3,2,1,0:T(8,128)(2,1)S(1)}, u32[]{:S(2)}, u32[]{:S(2)}) %collective-permute-start.9) | collective-permute-done | bytes 245792 | tf_op jit(solution)/shard_map/ppermute | solution.py:370
  186.0 0.1 fusion.1
  186.2 0.1 collective-permute-start.10
  186.3 7.9 %collective-permute-done.10.across_ref = bf16[144,8,128]{2,1,0:T(8,128)(2,1)S(1)} collective-permute-done((bf16[144,8,128]{2,1,0:T(8,128)(2,1)S(1)}, bf16[144,8,128]{2,1,0:T(8,128)(2,1)S(1)}, u32[]{:S(2)}, u32[]{:S(2)}) %collective-permute-start.10) | collective-permute-done | bytes 294944 | tf_op jit(solution)/shard_map/ppermute | solution.py:374
  194.2 1.6 collective-permute-start.11
  195.8 1.6 collective-permute-done.11.mate_ref
  197.4 0.8 copy-done.9
  198.2 9.9 %coarse_ff.1 = (f32[288,1024]{1,0:T(8,128)}, bf16[288,1024]{1,0:T(8,128)(2,1)}) custom-call(bf16[144,8,128]{2,1,0:T(8,128)(2,1)} %bitcast.45, bf16[144,8,128]{2,1,0:T(8,128)(2,1)} %copy-done.8, bf16[2,144,8,128]{3,2,1,0:T(8,128)(2,1)} %copy-done.9, f32[1,1024]{1,0:T(1,128)} %bitcast.57, bf16[4,512,1024]{2,1,0:T(8,128)(2,1)} %bitcast.47), custom_call_target="tpu_custom_call" | custom-call | tf_op jit(solution)/shard_map/coarse_ff/pallas_call | solution.py:305
  208.2 0.4 collective-permute-start.12
  208.5 1.8 collective-permute-done.12.mate_ref
  210.4 1.3 add_convert_fusion
  211.7 0.1 collective-permute-start.13
  211.8 8.2 %collective-permute-done.13.across_ref = bf16[144,1024]{1,0:T(8,128)(2,1)S(1)} collective-permute-done((bf16[144,1024]{1,0:T(8,128)(2,1)S(1)}, bf16[144,1024]{1,0:T(8,128)(2,1)S(1)}, u32[]{:S(2)}, u32[]{:S(2)}) %collective-permute-start.13) | collective-permute-done | bytes 294944 | tf_op jit(solution)/shard_map/ppermute | solution.py:374
  220.0 0.7 copy-done.15
  220.7 5.1 %blend.1 = (bf16[4,12,12,512]{3,2,1,0:T(8,128)(2,1)}, bf16[4,6,6,1024]{3,2,1,0:T(8,128)(2,1)}) custom-call(bf16[144,8,128]{2,1,0:T(8,128)(2,1)} %bitcast.46, f32[288,1024]{1,0:T(8,128)} %get-tuple-element.7.keep_ref, bf16[288,1024]{1,0:T(8,128)(2,1)} %copy-done.6, bf16[144,1024]{1,0:T(8,128)(2,1)} %copy-done.15, bf16[1024,2048]{1,0:T(8,128)(2,1)} %wu_ref.1, ...), custom_call_target="tpu_custom_call" | custom-call | tf_op jit(solution)/shard_map/blend/pallas_call | solution.py:348
  225.8 2.5 %copy.56 = bf16[4,12,12,512]{3,0,2,1:T(4,128)(2,1)} copy(bf16[4,12,12,512]{3,2,1,0:T(8,128)(2,1)} %get-tuple-element.14) | data formatting | bytes 1179648 | tf_op jit(solution)/shard_map/blend/pallas_call | solution.py:348
  228.2 0.9 copy.57
  (55 shorter events, 0.7 us)
Async XLA Ops:
  7.2 1.7 copy-start.13
  7.2 1.7 copy-start.17
  7.2 136.1 %all-gather.5.cloned.1.call-start = ((), (), s32[]{:S(2)}) async-start(), calls=%async_computation | async-start | bytes 13926400 | tf_op jit(solution)/shard_map/all_gather | solution.py:428
  8.8 1.1 copy-start.10
  8.9 1.4 copy-start.11
  9.9 185.9 %all-gather.7.cloned.1.call-start = ((), (), s32[]{:S(2)}) async-start(), calls=%async_computation.1 | async-start | bytes 5242880 | tf_op jit(solution)/shard_map/all_gather | solution.py:431
  10.2 1.3 copy-start.4
  11.6 9.8 %collective-permute-start = (bf16[4,12,11,512]{3,0,2,1:T(4,128)(2,1)S(1)}, bf16[4,12,11,512]{3,0,2,1:T(4,128)(2,1)S(1)}, u32[]{:S(2)}, u32[]{:S(2)}) collective-permute-start(bf16[4,12,11,512]{3,0,2,1:T(4,128)(2,1)S(1)} %slice.50), channel_id=1, source_target_pairs={{1,0},{2,1},{3,2},{4,3},{5,4},{6,5},{7,6},{8,7},{9,8},{10,9},{11,1... | collective-permute-start | bytes 1622024 | tf_op jit(solution)/shard_map/ppermute | solution.py:370
  13.3 9.3 %copy-start = (bf16[4,12,12,512]{3,2,1,0:T(8,128)(2,1)}, bf16[4,12,12,512]{3,2,1,0:T(8,128)(2,1)S(1)}, u32[]{:S(2)}) copy-start(bf16[4,12,12,512]{3,2,1,0:T(8,128)(2,1)S(1)} %copy.46.own_ref.x_ref) | copy-start | bytes 1769476
  13.3 15.1 %copy-start.18 = (s32[4]{0:T(128)S(1)}, s32[4]{0:T(128)}, u32[]{:S(2)}) copy-start(s32[4]{0:T(128)} %param.20) | copy-start | bytes 52
  13.3 17.0 %copy-start.5 = (bf16[512,1536]{1,0:T(8,128)(2,1)S(1)}, bf16[512,1536]{1,0:T(8,128)(2,1)}, u32[]{:S(2)}) copy-start(bf16[512,1536]{1,0:T(8,128)(2,1)} %param.22) | copy-start | bytes 4718596
  21.6 6.8 %copy-start.2 = (bf16[4,12,11,512]{3,2,1,0:T(8,128)(2,1)}, bf16[4,12,11,512]{3,2,1,0:T(8,128)(2,1)S(1)}, u32[]{:S(2)}) copy-start(bf16[4,12,11,512]{3,2,1,0:T(8,128)(2,1)S(1)} %copy.47.lon_ref) | copy-start | bytes 1622020
  22.6 25.2 %collective-permute-start.1 = (bf16[4,5,23,512]{3,2,1,0:T(8,128)(2,1)}, bf16[4,5,23,512]{3,2,1,0:T(8,128)(2,1)}, u32[]{:S(2)}, u32[]{:S(2)}) collective-permute-start(bf16[4,5,23,512]{3,2,1,0:T(8,128)(2,1)} %pad_maximum_fusion.3), channel_id=1, source_target_pairs={{16,0},{32,16},{48,32},{64,48},{80,64},{96,80},{112,96},{0,112},{1... | collective-permute-start | bytes 1413128 | tf_op jit(solution)/shard_map/ppermute | solution.py:370
  62.1 14.8 %slice-start = ((bf16[4,12,12,512]{3,2,1,0:T(8,128)(2,1)}), bf16[4,5,12,512]{3,2,1,0:T(8,128)(2,1)S(1)}, s32[]{:S(2)}) async-start(bf16[4,12,12,512]{3,2,1,0:T(8,128)(2,1)} %fine_attention.1.own_ref), calls=%async_computation.2 | async-start | bytes 655360 | tf_op jit(solution)/shard_map/slice | solution.py:456
  62.1 14.6 %collective-permute-start.2 = (bf16[4,12,11,512]{3,0,2,1:T(4,128)(2,1)S(1)}, bf16[4,12,11,512]{3,0,2,1:T(4,128)(2,1)S(1)}, u32[]{:S(2)}, u32[]{:S(2)}) collective-permute-start(bf16[4,12,11,512]{3,0,2,1:T(4,128)(2,1)S(1)} %copy.49), channel_id=1, source_target_pairs={{15,0},{0,1},{1,2},{2,3},{3,4},{4,5},{5,6},{6,7},{7,8},{8,9},{9,10... | collective-permute-start | bytes 1622024 | tf_op jit(solution)/shard_map/ppermute | solution.py:370
  76.9 21.9 %copy-start.3 = (bf16[4,12,11,512]{3,2,1,0:T(8,128)(2,1)}, bf16[4,12,11,512]{3,2,1,0:T(8,128)(2,1)S(1)}, u32[]{:S(2)}) copy-start(bf16[4,12,11,512]{3,2,1,0:T(8,128)(2,1)S(1)} %copy.51.lon_ref) | copy-start | bytes 1622020
  77.1 21.7 %collective-permute-start.3 = (bf16[4,5,23,512]{3,2,1,0:T(8,128)(2,1)S(1)}, bf16[4,5,23,512]{3,2,1,0:T(8,128)(2,1)S(1)}, u32[]{:S(2)}, u32[]{:S(2)}) collective-permute-start(bf16[4,5,23,512]{3,2,1,0:T(8,128)(2,1)S(1)} %pad_maximum_fusion.4), channel_id=1, source_target_pairs={{112,0},{0,16},{16,32},{32,48},{48,64},{64,80},{80,96},{96,112},{1... | collective-permute-start | bytes 1413128 | tf_op jit(solution)/shard_map/ppermute | solution.py:370
  98.8 0.8 copy-start.12
  113.6 11.0 %collective-permute-start.4 = (bf16[4,5,6,8,128]{4,3,2,1,0:T(8,128)(2,1)S(1)}, bf16[4,5,6,8,128]{4,3,2,1,0:T(8,128)(2,1)S(1)}, u32[]{:S(2)}, u32[]{:S(2)}) collective-permute-start(bf16[4,5,6,8,128]{4,3,2,1,0:T(8,128)(2,1)S(1)} %slice.56), channel_id=1, source_target_pairs={{16,0},{32,16},{48,32},{64,48},{80,64},{96,80},{112,96},{0,112},{1... | collective-permute-start | bytes 737288 | tf_op jit(solution)/shard_map/ppermute | solution.py:370
  124.7 2.0 collective-permute-start.5
  126.8 16.5 %copy-start.7 = (bf16[2,2,6,6,8,128]{5,4,3,2,1,0:T(8,128)(2,1)}, bf16[2,2,6,6,8,128]{5,4,3,2,1,0:T(8,128)(2,1)S(1)}, u32[]{:S(2)}) copy-start(bf16[2,2,6,6,8,128]{5,4,3,2,1,0:T(8,128)(2,1)S(1)} %pad_maximum_fusion.5.own_ref) | copy-start | bytes 884740
  126.8 16.5 %collective-permute-start.6 = (bf16[2,2,6,6,8,128]{5,4,3,2,1,0:T(8,128)(2,1)S(1)}, bf16[2,2,6,6,8,128]{5,4,3,2,1,0:T(8,128)(2,1)S(1)}, u32[]{:S(2)}, u32[]{:S(2)}) collective-permute-start(bf16[2,2,6,6,8,128]{5,4,3,2,1,0:T(8,128)(2,1)S(1)} %pad_maximum_fusion.5.own_ref), channel_id=1, source_target_pairs={{2,0},{3,1},{4,2},{5,3},{6,4},{7,5},{8,6},{9,7},{10,8},{11,9},{12,... | collective-permute-start | bytes 884744 | tf_op jit(solution)/shard_map/ppermute | solution.py:379
  143.3 0.7 copy-start.16
  158.3 10.0 %collective-permute-start.7 = (bf16[2,6,11,8,128]{4,3,2,1,0:T(8,128)(2,1)S(1)}, bf16[2,6,11,8,128]{4,3,2,1,0:T(8,128)(2,1)S(1)}, u32[]{:S(2)}, u32[]{:S(2)}) collective-permute-start(bf16[2,6,11,8,128]{4,3,2,1,0:T(8,128)(2,1)S(1)} %slice.66), channel_id=1, source_target_pairs={{14,0},{15,1},{0,2},{1,3},{2,4},{3,5},{4,6},{5,7},{6,8},{7,9},{8,1... | collective-permute-start | bytes 811016 | tf_op jit(solution)/shard_map/ppermute | solution.py:379
  169.1 3.1 %collective-permute-start.8 = (bf16[2,6,6,8,128]{4,3,2,1,0:T(8,128)(2,1)S(1)}, bf16[2,6,6,8,128]{4,3,2,1,0:T(8,128)(2,1)S(1)}, u32[]{:S(2)}, u32[]{:S(2)}) collective-permute-start(bf16[2,6,6,8,128]{4,3,2,1,0:T(8,128)(2,1)S(1)} %fusion.4), channel_id=1, source_target_pairs={{0,1},{1,0},{2,3},{3,2},{4,5},{5,4},{6,7},{7,6},{8,9},{9,8},{10,11... | collective-permute-start | bytes 442376 | tf_op jit(solution)/shard_map/ppermute | solution.py:374
  173.4 12.7 %collective-permute-start.9 = (bf16[4,5,6,8,128]{4,3,2,1,0:T(8,128)(2,1)S(1)}, bf16[4,5,6,8,128]{4,3,2,1,0:T(8,128)(2,1)S(1)}, u32[]{:S(2)}, u32[]{:S(2)}) collective-permute-start(bf16[4,5,6,8,128]{4,3,2,1,0:T(8,128)(2,1)S(1)} %slice.67), channel_id=1, source_target_pairs={{112,0},{0,16},{16,32},{32,48},{48,64},{64,80},{80,96},{96,112},{1... | collective-permute-start | bytes 737288 | tf_op jit(solution)/shard_map/ppermute | solution.py:370
  186.1 11.3 %copy-start.1 = (bf16[4,6,6,8,128]{4,3,2,1,0:T(8,128)(2,1)}, bf16[4,6,6,8,128]{4,3,2,1,0:T(8,128)(2,1)S(1)}, u32[]{:S(2)}) copy-start(bf16[4,6,6,8,128]{4,3,2,1,0:T(8,128)(2,1)S(1)} %fusion.1) | copy-start | bytes 884740
  186.2 7.9 %collective-permute-start.10 = (bf16[144,8,128]{2,1,0:T(8,128)(2,1)S(1)}, bf16[144,8,128]{2,1,0:T(8,128)(2,1)S(1)}, u32[]{:S(2)}, u32[]{:S(2)}) collective-permute-start(bf16[144,8,128]{2,1,0:T(8,128)(2,1)S(1)} %bitcast.43), channel_id=1, source_target_pairs={{0,8},{1,9},{2,10},{3,11},{4,12},{5,13},{6,14},{7,15},{8,0},{9,1},... | collective-permute-start | bytes 884744 | tf_op jit(solution)/shard_map/ppermute | solution.py:374
  194.1 3.3 %copy-start.8 = (bf16[144,8,128]{2,1,0:T(8,128)(2,1)}, bf16[144,8,128]{2,1,0:T(8,128)(2,1)S(1)}, u32[]{:S(2)}) copy-start(bf16[144,8,128]{2,1,0:T(8,128)(2,1)S(1)} %collective-permute-done.10.across_ref) | copy-start | bytes 884740
  194.2 3.3 %collective-permute-start.11 = (bf16[2,144,8,128]{3,2,1,0:T(8,128)(2,1)S(1)}, bf16[2,144,8,128]{3,2,1,0:T(8,128)(2,1)S(1)}, u32[]{:S(2)}, u32[]{:S(2)}) collective-permute-start(bf16[2,144,8,128]{3,2,1,0:T(8,128)(2,1)S(1)} %pad_maximum_fusion.2), channel_id=1, source_target_pairs={{0,1},{1,0},{2,3},{3,2},{4,5},{5,4},{6,7},{7,6},{8,9},{9,8},{10,11... | collective-permute-start | bytes 1769480 | tf_op jit(solution)/shard_map/ppermute | solution.py:374
  197.4 0.8 copy-start.9
  208.2 2.2 collective-permute-start.12
  210.4 9.7 %copy-start.6 = (bf16[288,1024]{1,0:T(8,128)(2,1)}, bf16[288,1024]{1,0:T(8,128)(2,1)S(1)}, u32[]{:S(2)}) copy-start(bf16[288,1024]{1,0:T(8,128)(2,1)S(1)} %collective-permute-done.12.mate_ref) | copy-start | bytes 1769476
  211.7 8.3 %collective-permute-start.13 = (bf16[144,1024]{1,0:T(8,128)(2,1)S(1)}, bf16[144,1024]{1,0:T(8,128)(2,1)S(1)}, u32[]{:S(2)}, u32[]{:S(2)}) collective-permute-start(bf16[144,1024]{1,0:T(8,128)(2,1)S(1)} %add_convert_fusion), channel_id=1, source_target_pairs={{0,8},{1,9},{2,10},{3,11},{4,12},{5,13},{6,14},{7,15},{8,0},{9,1},... | collective-permute-start | bytes 884744 | tf_op jit(solution)/shard_map/ppermute | solution.py:374
  220.0 0.7 copy-start.15
  225.8 2.5 %copy-start.14 = (bf16[4,6,6,1024]{3,2,1,0:T(8,128)(2,1)S(1)}, bf16[4,6,6,1024]{3,2,1,0:T(8,128)(2,1)}, u32[]{:S(2)}) copy-start(bf16[4,6,6,1024]{3,2,1,0:T(8,128)(2,1)} %get-tuple-element.15) | copy-start | bytes 884740
Sparse Core Ops, SparseCore 0:
  10.0 104.8 all-gather.4
  116.6 52.0 all-gather.6
where the time goes:
time: 236 us
  waiting for transfers between devices  112 us (47%)
  Pallas kernels  53.7 us (23%)
  starting transfers between devices  25.6 us (11%)
  between operations  19.6 us (8%)
  local copies, waits for them, and re-layouts  16.1 us (7%)
  other arithmetic  8.94 us (4%)
    ppermute x6, waiting for transfers between devices, shifted(): return lax.ppermute(block, axis, route)  68.4 us
    ppermute x2, waiting for transfers between devices, chip_shifted(): lax.ppermute(block, 'lon', [((i - 2 * distance) % count, i) for i in rang...  22.1 us
    ppermute x6, waiting for transfers between devices, swapped(): lax.ppermute(block, 'lon', [(i, i ^ bit) for i in range(lax.axis_size('lo...  21.5 us
    ppermute x6, starting transfers between devices, shifted(): return lax.ppermute(block, axis, route)  16.5 us
    pallas_call x1, Pallas kernels, coarse_attention(): pl.pallas_call(coarse_attn_kernel, grid=(8,), out_shape=jax.ShapeDtypeStr...  13.3 us
    pallas_call x1, Pallas kernels, fine_post(): pl.pallas_call(fine_post_kernel, out_shape=(jax.ShapeDtypeStruct((4, WT,...  13 us
    pallas_call x1, Pallas kernels, fine_attention(): pl.pallas_call(fine_attn_kernel, out_shape=jax.ShapeDtypeStruct((4, 12, 1...  12.4 us
    pallas_call x1, Pallas kernels, coarse_ff(): pl.pallas_call(coarse_ff_kernel, grid=(4,), out_shape=(jax.ShapeDtypeStru...  9.91 us
  transfers between devices with their start and end apart: 16, of which 14 were waited for; matrix products, arithmetic and copies ran while one was open for 6% of the time, Pallas kernels for 16%

commit v1 on v0

--- a/solution.py
+++ b/solution.py
@@ -69,22 +69,42 @@
     return jnp.where(reg(0) == reg(1), 0.0, NEG).astype(F32)
 
 
-def fine_attn_kernel(sc_ref, own_ref, lon_ref, lat_ref, gain_ref, w_ref, bias_ref, out_ref, ext, xw, q_s, k_s, v_s, mask_s, o_s):
-    s0 = sc_ref[0]
-    s1 = sc_ref[1]
+def fill_frame(sc_ref, own_ref, lon_ref, lat_ref, ext, ahead):
+    lat_row = jnp.where(sc_ref[4] == ahead, 15, 0)
+    after = sc_ref[5] == ahead
     for l in range(4):
         for r in range(12):
-            ext[l, r, 0:12] = own_ref[l, r].astype(F32)
-            ext[l, r, 12:23] = lon_ref[l, r].astype(F32)
-        for r in range(5):
-            ext[l, 12 + r, 0:23] = lat_ref[l, r].astype(F32)
+            ext[l, 3 + r, 6:18] = own_ref[l, r].astype(F32)
+        for r in range(3):
+            ext[l, lat_row + r, 6:18] = lat_ref[l, r, 0:12].astype(F32)
+
+    def edge(cols):
+        for l in range(4):
+            for r in range(12):
+                ext[l, 3 + r, cols] = lon_ref[l, r].astype(F32)
+            for r in range(3):
+                ext[l, lat_row + r, cols] = lat_ref[l, r, 12:18].astype(F32)
+
+    @pl.when(after)
+    def _():
+        edge(slice(18, 24))
+
+    @pl.when(jnp.logical_not(after))
+    def _():
+        edge(slice(0, 6))
+
+
+def fine_attn_kernel(sc_ref, own_ref, lon_ref, lat_ref, gain_ref, w_ref, bias_ref, out_ref, ext, xw, q_s, k_s, v_s, mask_s, o_s):
+    row0 = 3 + sc_ref[0]
+    turn = 18 - sc_ref[1]
+    fill_frame(sc_ref, own_ref, lon_ref, lat_ref, ext, 1)
     for dp in range(2):
         for lr in range(2):
             for a in range(2):
                 for b in range(6):
                     row = ((dp * 2 + lr) * 12 + a * 6 + b) * 12
-                    full = ext[dp * 2 + a, s0 + lr * 6 + b]
-                    xw[row : row + 12] = pltpu.roll(full, 24 - s1, 0)[0:12]
+                    full = ext[dp * 2 + a, row0 + lr * 6 + b]
+                    xw[row : row + 12] = pltpu.roll(full, turn, 0)[0:12]
     gain = gain_ref[...]
 
     def project(i, _):
@@ -98,7 +118,7 @@
     lax.fori_loop(0, 4, project, 0)
 
     def window(i, _):
-        thr = jnp.where(i % 2 == 1, sc_ref[2], 1000)
+        thr = jnp.where(i % 2 == sc_ref[3], sc_ref[2], 1000)
         mask_s[...] = region_mask(thr)
         rows = pl.ds(i * WT, WT)
         for j in range(4):
@@ -129,7 +149,7 @@
         in_specs=full_spec(7, (0,)),
         out_specs=pl.BlockSpec(memory_space=pltpu.VMEM),
         scratch_shapes=[
-            pltpu.VMEM((4, 17, 24, 512), F32),
+            pltpu.VMEM((4, 18, 24, 512), F32),
             pltpu.VMEM((576, 512), F32),
             pltpu.VMEM((576, 512), BF),
             pltpu.VMEM((576, 512), BF),
@@ -143,17 +163,14 @@
 
 
 def fine_post_kernel(sc_ref, own_ref, lon_ref, lat_ref, x_ref, wo_ref, g_ref, we_ref, wr_ref, mg_ref, wm_ref, fs_ref, ci_ref, ext, xf, mf, xp, mp, tiles):
-    r0 = 5 - sc_ref[0]
-    turn = 16 + sc_ref[1]
+    r0 = 3 - sc_ref[0]
+    turn = (18 + sc_ref[1]) % 24
+    fill_frame(sc_ref, own_ref, lon_ref, lat_ref, ext, 0)
     for l in range(4):
         for r in range(12):
-            ext[l, 5 + r, 16:28] = own_ref[l, r].astype(F32)
-            ext[l, 5 + r, 5:16] = lon_ref[l, r].astype(F32)
             own_x = x_ref[l, r].astype(F32)
             for c in range(4):
                 xf[c, l, r, 0:12] = own_x[:, 128 * c : 128 * c + 128]
-        for r in range(5):
-            ext[l, r, 5:28] = lat_ref[l, r].astype(F32)
     for l in range(4):
         for r in range(12):
             turned = pltpu.roll(ext[l, r0 + r], turn, 0)[0:16]
@@ -199,7 +216,7 @@
         in_specs=full_spec(11, (0,)),
         out_specs=(pl.BlockSpec(memory_space=pltpu.VMEM), pl.BlockSpec(memory_space=pltpu.VMEM)),
         scratch_shapes=[
-            pltpu.VMEM((4, 17, 32, 512), F32),
+            pltpu.VMEM((4, 18, 24, 512), F32),
             pltpu.VMEM((4, 4, 12, 16, 128), F32),
             pltpu.VMEM((4, 4, 12, 16, 128), F32),
             pltpu.VMEM((576, 512), F32),
@@ -216,20 +233,22 @@
 
     @pl.when(j == 0)
     def _():
-        s3 = sc_ref[3]
-        for half in range(2):
-            for a in range(2):
-                ext[a, :, 6 * half : 6 * half + 6] = own_ref[half, a].astype(F32)
-                ext[a, :, 12 + 6 * half : 18 + 6 * half] = next_ref[half, a].astype(F32)
+        first = 6 + sc_ref[6]
+        edge = jnp.where(sc_ref[7] == 1, 18, 0)
+        for a in range(2):
+            for half in range(2):
+                ext[a, :, 6 + 6 * half : 12 + 6 * half] = own_ref[half, a].astype(F32)
+            for b in range(6):
+                ext[a, b, pl.ds(edge, 6)] = next_ref[a, b].astype(F32)
         for a in range(2):
             for b in range(6):
                 row = (a * 6 + b) * 96
-                tiles[row : row + 96] = ext[a, b, pl.ds(s3, 12)].reshape(96, 128)
+                tiles[row : row + 96] = ext[a, b, pl.ds(first, 12)].reshape(96, 128)
         for c, part in enumerate(tiles_to_rows(tiles, 0, WT)):
             xf[:, 128 * c : 128 * c + 128] = part
         xn[...] = norm_rows(xf[...], gain_ref[...]).astype(BF)
         acc[...] = xf[...]
-        mask_s[...] = region_mask(sc_ref[4])
+        mask_s[...] = region_mask(sc_ref[8])
 
     def rows_of(first, count):
         return jnp.concatenate([g_ref[0, first : first + count], g_ref[1, first : first + count]], axis=0)
@@ -377,6 +396,40 @@
 def chip_shifted(block, distance):
     count = lax.axis_size("lon")
     return lax.ppermute(block, "lon", [((i - 2 * distance) % count, i) for i in range(count)])
+
+
+def fine_shift_lon(block, distance):
+    return shifted(block, "lon", distance)
+
+
+def fine_shift_lat(block, distance):
+    return shifted(block, "lat", distance)
+
+
+def split_shift(shift, window):
+    ahead = shift <= window // 2
+    return ahead, jnp.where(ahead, shift, shift - window)
+
+
+def one_way(ahead, block, dim, width, move, to_frame):
+    low = lambda v: lax.slice_in_dim(v, 0, width, axis=dim)
+    high = lambda v: lax.slice_in_dim(v, v.shape[dim] - width, v.shape[dim], axis=dim)
+    if to_frame:
+        return lax.cond(ahead, lambda v: move(low(v), -1), lambda v: move(high(v), 1), block)
+    return lax.cond(ahead, lambda v: move(high(v), 1), lambda v: move(low(v), -1), block)
+
+
+def edge_rows(ahead, block, piece, to_frame):
+    low = lambda v: jnp.concatenate([v[0][:, :3], v[1][:, :3]], axis=2)
+    high = lambda v: jnp.concatenate([v[0][:, -3:], v[1][:, -3:]], axis=2)
+    pair = (block, piece)
+    if to_frame:
+        return lax.cond(
+            ahead, lambda v: fine_shift_lat(low(v), -1), lambda v: fine_shift_lat(high(v), 1), pair
+        )
+    return lax.cond(
+        ahead, lambda v: fine_shift_lat(high(v), 1), lambda v: fine_shift_lat(low(v), -1), pair
+    )
 
 
 def in_order(core, mine, other):
@@ -429,56 +482,66 @@
     ff_pack = jnp.concatenate([coarse_expand.T, coarse_reduce], axis=0)
     rings = [[z * 8 + y * 2 + c for y in range(4)] for z in range(2) for c in range(2)]
     ff_all = lax.all_gather(ff_pack, "lon", axis=0, tiled=False, axis_index_groups=rings)
-    lon_ahead = shifted(fine_field[:, :, : WW - 1], "lon", -1)
-    lat_ahead = shifted(
-        jnp.concatenate([fine_field[:, : WL - 1], lon_ahead[:, : WL - 1]], axis=2), "lat", -1
-    )
+    fine_up, fine_row = split_shift(fine_lat, WL)
+    fine_right, fine_col = split_shift(fine_lon, WW)
+    coarse_up, coarse_row = split_shift(coarse_lat, WL)
+    coarse_right, coarse_col = split_shift(coarse_lon, WW)
+    lon_piece = one_way(fine_right, fine_field, 2, 6, fine_shift_lon, True)
+    lat_piece = edge_rows(fine_up, fine_field, lon_piece, True)
     half_rows = lat_rows // 2
     half_cols = lon_cols // 2
-    last_band = lat_index == lat_count - 1
+
+
+    def threshold(up, shift):
+        band = jnp.where(up, lat_count - 1, 0)
+        return jnp.where(lat_index == band, 12 * (WL - shift), 1000)
+
     scalars = jnp.stack(
         [
-            fine_lat,
-            fine_lon,
-            jnp.where(last_band, 12 * (WL - fine_lat), 1000),
-            coarse_lon,
-            jnp.where(last_band, 12 * (WL - coarse_lat), 1000),
+            fine_row,
+            fine_col,
+            threshold(fine_up, fine_lat),
+            fine_up.astype(jnp.int32),
+            fine_up.astype(jnp.int32),
+            fine_right.astype(jnp.int32),
+            coarse_col,
+            coarse_right.astype(jnp.int32),
+            threshold(coarse_up, coarse_lat),
         ]
     )
     triple_heads = fine_triple.reshape(channels, -1, 3, 32).transpose(2, 0, 1, 3)
     triple_heads = triple_heads.reshape(3, channels, channels)
     mixed_fine = fine_attention(
-        scalars, fine_field, lon_ahead, lat_ahead, fine_prenorm[None], triple_heads, fine_bias
-    )
-    lon_behind = shifted(mixed_fine[:, :, lon_cols - WW + 1 :], "lon", 1)
-    tail = lat_rows - WL + 1
-    lat_behind = shifted(
-        jnp.concatenate([lon_behind[:, tail:], mixed_fine[:, tail:]], axis=2), "lat", 1
-    )
+        scalars, fine_field, lon_piece, lat_piece, fine_prenorm[None], triple_heads, fine_bias
+    )
+    lon_piece = one_way(fine_right, mixed_fine, 2, 6, fine_shift_lon, False)
+    lat_piece = edge_rows(fine_up, mixed_fine, lon_piece, False)
     fine_state, coarse_own = fine_post(
-        scalars, mixed_fine, lon_behind, lat_behind, fine_field, fine_output, fine_midnorm[None],
+        scalars, mixed_fine, lon_piece, lat_piece, fine_field, fine_output, fine_midnorm[None],
         fine_expand, fine_reduce, merge_gain[None], merge_weight,
     )
-    rows_ahead = shifted(coarse_own[:, : WL - 1], "lat", -1)
+    rows_piece = one_way(coarse_up, coarse_own, 1, 3, fine_shift_lat, True)
     framed = lax.dynamic_slice_in_dim(
-        jnp.concatenate([coarse_own, rows_ahead], axis=1), coarse_lat, half_rows, axis=1
+        jnp.concatenate([rows_piece, coarse_own, rows_piece], axis=1), 3 + coarse_row, half_rows, axis=1
     )
     mine = lax.dynamic_slice_in_dim(framed, 2 * core, 2, axis=0)
     other = swapped(lax.dynamic_slice_in_dim(framed, 2 - 2 * core, 2, axis=0), 1)
     chip = in_order(core, mine, other)
-    chip_ahead = chip_shifted(chip, -1)
-    mid_framed = coarse_attention(scalars, chip, chip_ahead, coarse_prenorm[None], attn_all)
-    cols_behind = chip_shifted(mid_framed[:, :, 1:], 1)
-    spread = jnp.concatenate([cols_behind, mid_framed], axis=2)
-    first = WW - 1 - coarse_lon
+    chip_piece = lax.cond(
+        coarse_right, lambda v: chip_shifted(v[0], -1), lambda v: chip_shifted(v[1], 1), chip
+    )
+    mid_framed = coarse_attention(scalars, chip, chip_piece, coarse_prenorm[None], attn_all)
+    cols_piece = one_way(coarse_right, mid_framed, 2, 6, chip_shifted, False)
+    spread = jnp.concatenate([cols_piece, mid_framed, cols_piece], axis=2)
+    first = 6 - coarse_col
     mine = lax.dynamic_slice_in_dim(spread, first + half_cols * core, half_cols, axis=2)
     other = swapped(
         lax.dynamic_slice_in_dim(spread, first + half_cols * (1 - core), half_cols, axis=2), 1
     )
     levels_all = in_order(core, mine, other).reshape(levels, half_rows, half_cols, 8, 128)
-    rows_behind = shifted(levels_all[:, 1:], "lat", 1)
+    rows_piece = one_way(coarse_up, levels_all, 1, 3, fine_shift_lat, False)
     mid_own = lax.dynamic_slice_in_dim(
-        jnp.concatenate([rows_behind, levels_all], axis=1), WL - 1 - coarse_lat, half_rows, axis=1
+        jnp.concatenate([rows_piece, levels_all, rows_piece], axis=1), 3 - coarse_row, half_rows, axis=1
     )
     mid_own = mid_own.reshape(WT, 8, 128)
     across = swapped(mid_own, 8)

time: 236 us -> 218 us (0.924)
  waiting for transfers between devices: 112 us -> 104 us
  starting transfers between devices: 25.6 us -> 18.7 us
  Pallas kernels: 53.7 us -> 50.3 us
  between operations: 19.6 us -> 22.8 us
    ppermute x6, waiting for transfers between devices: 68.4 us -> 59.1 us  [shifted(): return lax.ppermute(block, axis, route)]
    ppermute x6, starting transfers between devices: 16.5 us -> 10.7 us  [shifted(): return lax.ppermute(block, axis, route)]
    ppermute x2, waiting for transfers between devices: 22.1 us -> 25.2 us  [chip_shifted(): lax.ppermute(block, 'lon', [((i - 2 * distance) % count, i) for i in rang...]
    slice x12 -> x10, local copies, waits for them, and re-layouts: 4.75 us -> 2.61 us  [the longest x2 0.92 us: edge_rows(): high = lambda v: jnp.concatenate([v[0][:, -3:], v[1][:, -3:]], axis=2)]
    unnamed x42 -> x29, local copies, waits for them, and re-layouts: 5.33 us -> 3.7 us
where the time goes in v1:
time: 218 us; the launch traced here: 219 us
  waiting for transfers between devices  104 us (48%)
  Pallas kernels  50.3 us (23%)
  between operations  22.8 us (10%)
  starting transfers between devices  18.7 us (9%)
  local copies, waits for them, and re-layouts  14.2 us (7%)
  other arithmetic  8.49 us (4%)
    ppermute x6, waiting for transfers between devices, shifted(): return lax.ppermute(block, axis, route)  59.1 us
    ppermute x2, waiting for transfers between devices, chip_shifted(): lax.ppermute(block, 'lon', [((i - 2 * distance) % count, i) for i in rang...  25.2 us
    ppermute x6, waiting for transfers between devices, swapped(): lax.ppermute(block, 'lon', [(i, i ^ bit) for i in range(lax.axis_size('lo...  19.6 us
    pallas_call x1, Pallas kernels, coarse_attention(): pl.pallas_call(coarse_attn_kernel, grid=(8,), out_shape=jax.ShapeDtypeStr...  12.5 us
    pallas_call x1, Pallas kernels, fine_post(): pl.pallas_call(fine_post_kernel, out_shape=(jax.ShapeDtypeStruct((4, WT,...  11.8 us
    pallas_call x1, Pallas kernels, fine_attention(): pl.pallas_call(fine_attn_kernel, out_shape=jax.ShapeDtypeStruct((4, 12, 1...  11 us
    ppermute x6, starting transfers between devices, shifted(): return lax.ppermute(block, axis, route)  10.7 us
    pallas_call x1, Pallas kernels, coarse_ff(): pl.pallas_call(coarse_ff_kernel, grid=(4,), out_shape=(jax.ShapeDtypeStru...  9.89 us
  transfers between devices with their start and end apart: 16, of which 14 were waited for; matrix products, arithmetic and copies ran while one was open for 6% of the time, Pallas kernels for 16%

profile of v1, /device:TPU:1, one launch (start us, length us, event | category | flops | bytes accessed | tf_op | source)
XLA Modules:
  0.0 218.6 jit_solution(3913007644563825431)
XLA Ops:
  7.2 1.0 fusion.4
  8.3 0.3 copy.42
  8.6 0.2 reshape.35
  8.9 0.9 pad_maximum_fusion.5
  9.9 0.2 copy.43
  10.2 0.2 copy-done.7
  10.3 1.0 pad_maximum_fusion.4
  11.4 0.6 fusion.5
  19.9 0.1 copy.38.own_ref.x_ref
  20.1 16.8 %conditional.8 = (bf16[4,12,6,512]{3,2,1,0:T(8,128)(2,1)}) conditional(s32[]{:T(128)} %convert_element_type.32, bf16[4,12,12,512]{3,2,1,0:T(8,128)(2,1)S(1)} %copy.38.own_ref.x_ref, bf16[4,12,12,512]{3,2,1,0:T(8,128)(2,1)S(1)} %copy.38.own_ref.x_ref), branch_computations={%region_0.1_spmd, %region_1.2_spmd} | conditional | bytes 1769520 | solution.py:418
  20.1 1.5 collective-permute-start.1
  21.6 15.2 %collective-permute-done.1 = bf16[4,12,6,512]{3,2,1,0:T(8,128)(2,1)} collective-permute-done((bf16[4,12,6,512]{3,2,1,0:T(8,128)(2,1)S(1)}, bf16[4,12,6,512]{3,2,1,0:T(8,128)(2,1)}, u32[]{:S(2)}, u32[]{:S(2)}) %collective-permute-start.1) | collective-permute-done | bytes 294944 | tf_op jit(solution)/shard_map/cond/branch_1_fun/ppermute | solution.py:389
  36.8 1.6 copy.36
  38.4 1.5 copy.37
  40.0 1.6 copy.39.w_ref
  41.5 15.9 %conditional.9 = (bf16[4,3,18,512]{3,2,1,0:T(8,128)(2,1)}) conditional(s32[]{:T(128)} %convert_element_type.16, (bf16[4,12,12,512]{3,0,2,1:T(4,128)(2,1)S(1)}, bf16[4,12,6,512]{3,2,1,0:T(8,128)(2,1)}) %tuple.89, (bf16[4,12,12,512]{3,0,2,1:T(4,128)(2,1)S(1)}, bf16[4,12,6,512]{3,2,1,0:T(8,128)(2,1)}) %tuple.90), branch_computations={%region_2.3_spmd, %region_3.4_spmd} | conditional | flops 442368 | bytes 2949168 | solution.py:427
  41.5 0.1 copy.34
  41.7 0.9 slice.51
  42.7 3.6 %collective-permute-start.12 = (bf16[4,3,18,512]{3,2,1,0:T(8,128)(2,1)S(1)}, bf16[4,3,18,512]{3,2,1,0:T(8,128)(2,1)}, u32[]{:S(2)}, u32[]{:S(2)}) collective-permute-start(bf16[4,3,18,512]{3,2,1,0:T(8,128)(2,1)S(1)} %pad_maximum_fusion), channel_id=1, source_target_pairs={{112,0},{0,16},{16,32},{32,48},{48,64},{64,80},{80,96},{96,112},{1... | collective-permute-start | bytes 663560 | tf_op jit(solution)/shard_map/cond/branch_0_fun/ppermute | solution.py:389
  46.3 11.1 %collective-permute-done.12 = bf16[4,3,18,512]{3,2,1,0:T(8,128)(2,1)} collective-permute-done((bf16[4,3,18,512]{3,2,1,0:T(8,128)(2,1)S(1)}, bf16[4,3,18,512]{3,2,1,0:T(8,128)(2,1)}, u32[]{:S(2)}, u32[]{:S(2)}) %collective-permute-start.12) | collective-permute-done | bytes 221216 | tf_op jit(solution)/shard_map/cond/branch_0_fun/ppermute | solution.py:389
  57.4 0.7 stack.72.sc_ref
  58.1 11.0 %fine_attention.1.own_ref = bf16[4,12,12,512]{3,2,1,0:T(8,128)(2,1)S(1)} custom-call(s32[9]{0:T(128)} %stack.72.sc_ref, bf16[4,12,12,512]{3,2,1,0:T(8,128)(2,1)S(1)} %copy.38.own_ref.x_ref, bf16[4,12,6,512]{3,2,1,0:T(8,128)(2,1)} %get-tuple-element.92.lon_ref, bf16[4,3,18,512]{3,2,1,0:T(8,128)(2,1)} %get-tuple-element.93.lat_ref, f32[1,512]{1,0:T(1,128)} %bitcast.64, ...), custom_call_target="tpu_custom_call" | custom-call | tf_op jit(solution)/shard_map/fine_attention/pallas_call | solution.py:146
  69.2 5.6 %conditional.10 = (bf16[4,12,6,512]{3,2,1,0:T(8,128)(2,1)}) conditional(s32[]{:T(128)} %convert_element_type.32, bf16[4,12,12,512]{3,2,1,0:T(8,128)(2,1)S(1)} %fine_attention.1.own_ref, bf16[4,12,12,512]{3,2,1,0:T(8,128)(2,1)S(1)} %fine_attention.1.own_ref), branch_computations={%region_4.5_spmd, %region_5.6_spmd} | conditional | bytes 1769520 | solution.py:419
  69.2 0.1 slice.55
  69.4 5.4 %collective-permute-done.3 = bf16[4,12,6,512]{3,2,1,0:T(8,128)(2,1)} collective-permute-done((bf16[4,12,6,512]{3,2,1,0:T(8,128)(2,1)S(1)}, bf16[4,12,6,512]{3,2,1,0:T(8,128)(2,1)}, u32[]{:S(2)}, u32[]{:S(2)}) %collective-permute-start.3) | collective-permute-done | bytes 294944 | tf_op jit(solution)/shard_map/cond/branch_1_fun/ppermute | solution.py:389
  74.8 18.8 %conditional.11 = (bf16[4,3,18,512]{3,2,1,0:T(8,128)(2,1)}) conditional(s32[]{:T(128)} %convert_element_type.16, (bf16[4,12,12,512]{3,2,1,0:T(8,128)(2,1)S(1)}, bf16[4,12,6,512]{3,2,1,0:T(8,128)(2,1)}) %tuple.56, (bf16[4,12,12,512]{3,2,1,0:T(8,128)(2,1)S(1)}, bf16[4,12,6,512]{3,2,1,0:T(8,128)(2,1)}) %tuple.56), branch_computations={%region_6.7_spmd, %region_7.8_spmd} | conditional | flops 442368 | bytes 1769520 | solution.py:430
  74.8 0.9 slice.57
  75.8 5.3 %collective-permute-start.14 = (bf16[4,3,18,512]{3,2,1,0:T(8,128)(2,1)S(1)}, bf16[4,3,18,512]{3,2,1,0:T(8,128)(2,1)}, u32[]{:S(2)}, u32[]{:S(2)}) collective-permute-start(bf16[4,3,18,512]{3,2,1,0:T(8,128)(2,1)S(1)} %pad_maximum_fusion.2), channel_id=1, source_target_pairs={{16,0},{32,16},{48,32},{64,48},{80,64},{96,80},{112,96},{0,112},{1... | collective-permute-start | bytes 663560 | tf_op jit(solution)/shard_map/cond/branch_0_fun/ppermute | solution.py:389
  81.1 12.5 %collective-permute-done.14 = bf16[4,3,18,512]{3,2,1,0:T(8,128)(2,1)} collective-permute-done((bf16[4,3,18,512]{3,2,1,0:T(8,128)(2,1)S(1)}, bf16[4,3,18,512]{3,2,1,0:T(8,128)(2,1)}, u32[]{:S(2)}, u32[]{:S(2)}) %collective-permute-start.14) | collective-permute-done | bytes 221216 | tf_op jit(solution)/shard_map/cond/branch_0_fun/ppermute | solution.py:389
  94.2 11.8 %fine_post.1 = (bf16[4,144,512]{2,1,0:T(8,128)(2,1)}, bf16[4,6,6,8,128]{4,3,2,1,0:T(8,128)(2,1)S(1)}) custom-call(s32[9]{0:T(128)} %stack.72.sc_ref, bf16[4,12,12,512]{3,2,1,0:T(8,128)(2,1)S(1)} %fine_attention.1.own_ref, bf16[4,12,6,512]{3,2,1,0:T(8,128)(2,1)} %get-tuple-element.94.lon_ref, bf16[4,3,18,512]{3,2,1,0:T(8,128)(2,1)} %get-tuple-element.95.lat_ref, ...), custom_call_target="tpu_custom_call" | custom-call | tf_op jit(solution)/shard_map/fine_post/pallas_call | solution.py:213
  105.9 8.4 %conditional.12 = (bf16[4,3,6,8,128]{4,3,2,1,0:T(8,128)(2,1)}) conditional(s32[]{:T(128)} %convert_element_type.14, bf16[4,6,6,8,128]{4,3,2,1,0:T(8,128)(2,1)S(1)} %get-tuple-element.66, bf16[4,6,6,8,128]{4,3,2,1,0:T(8,128)(2,1)S(1)} %get-tuple-element.66), branch_computations={%region_8.9_spmd, %region_9.10_spmd} | conditional | bytes 884784 | solution.py:418
  106.1 8.3 %collective-permute-done.4 = bf16[4,3,6,8,128]{4,3,2,1,0:T(8,128)(2,1)} collective-permute-done((bf16[4,3,6,8,128]{4,3,2,1,0:T(8,128)(2,1)S(1)}, bf16[4,3,6,8,128]{4,3,2,1,0:T(8,128)(2,1)}, u32[]{:S(2)}, u32[]{:S(2)}) %collective-permute-start.4) | collective-permute-done | bytes 147488 | tf_op jit(solution)/shard_map/cond/branch_0_fun/ppermute | solution.py:389
  114.4 1.1 pad_maximum_fusion.6
  115.5 0.1 collective-permute-start.16
  115.6 1.3 collective-permute-done.16
  117.0 18.0 %conditional.13 = (bf16[2,6,6,8,128]{4,3,2,1,0:T(8,128)(2,1)}) conditional(s32[]{:T(128)} %convert_element_type.15, bf16[2,6,6,8,128]{4,3,2,1,0:T(8,128)(2,1)S(1)} %get-tuple-element.85, bf16[2,6,6,8,128]{4,3,2,1,0:T(8,128)(2,1)S(1)} %get-tuple-element.84), branch_computations={%region_10.11_spmd, %region_11.12_spmd} | conditional | bytes 589872 | solution.py:530
  117.0 17.9 %collective-permute-done.6 = bf16[2,6,6,8,128]{4,3,2,1,0:T(8,128)(2,1)} collective-permute-done((bf16[2,6,6,8,128]{4,3,2,1,0:T(8,128)(2,1)S(1)}, bf16[2,6,6,8,128]{4,3,2,1,0:T(8,128)(2,1)}, u32[]{:S(2)}, u32[]{:S(2)}) %collective-permute-start.6) | collective-permute-done | bytes 147488 | tf_op jit(solution)/shard_map/cond/branch_0_fun/ppermute | solution.py:398
  134.9 0.7 pad_maximum_fusion.9.own_ref
  135.7 12.5 %coarse_attention.1 = bf16[2,6,12,8,128]{4,3,2,1,0:T(8,128)(2,1)S(1)} custom-call(s32[9]{0:T(128)} %stack.72.sc_ref, bf16[2,2,6,6,8,128]{5,4,3,2,1,0:T(8,128)(2,1)} %pad_maximum_fusion.9.own_ref, bf16[2,6,6,8,128]{4,3,2,1,0:T(8,128)(2,1)} %get-tuple-element.97.next_ref, f32[1,1024]{1,0:T(1,128)} %bitcast.62, bf16[16,400,1024]{2,1,0:T(8,128)(2,1)} %bitcast.44), custom_call_target="tpu_custom_call" | custom-call | tf_op jit(solution)/shard_map/coarse_attention/pallas_call | solution.py:279
  148.2 8.7 %conditional.14 = (bf16[2,6,6,8,128]{4,3,2,1,0:T(8,128)(2,1)}) conditional(s32[]{:T(128)} %convert_element_type.15, bf16[2,6,12,8,128]{4,3,2,1,0:T(8,128)(2,1)S(1)} %coarse_attention.1, bf16[2,6,12,8,128]{4,3,2,1,0:T(8,128)(2,1)S(1)} %coarse_attention.1), branch_computations={%region_12.13_spmd, %region_13.14_spmd} | conditional | bytes 884784 | solution.py:419
  148.2 1.4 collective-permute-start.8
  149.6 7.3 %collective-permute-done.8 = bf16[2,6,6,8,128]{4,3,2,1,0:T(8,128)(2,1)} collective-permute-done((bf16[2,6,6,8,128]{4,3,2,1,0:T(8,128)(2,1)S(1)}, bf16[2,6,6,8,128]{4,3,2,1,0:T(8,128)(2,1)}, u32[]{:S(2)}, u32[]{:S(2)}) %collective-permute-start.8) | collective-permute-done | bytes 147488 | tf_op jit(solution)/shard_map/cond/branch_0_fun/ppermute | solution.py:398
  156.9 1.1 pad_maximum_fusion.7
  158.0 1.8 collective-permute-start.17
  159.9 1.0 collective-permute-done.17
  160.9 6.8 %conditional.15 = (bf16[4,3,6,8,128]{4,3,2,1,0:T(8,128)(2,1)}) conditional(s32[]{:T(128)} %convert_element_type.14, bf16[4,6,6,8,128]{4,3,2,1,0:T(8,128)(2,1)S(1)} %bitcast.52, bf16[4,6,6,8,128]{4,3,2,1,0:T(8,128)(2,1)S(1)} %bitcast.53), branch_computations={%region_14.15_spmd, %region_15.16_spmd} | conditional | bytes 884784 | solution.py:419
  161.0 0.2 collective-permute-start.10
  161.1 6.6 %collective-permute-done.10 = bf16[4,3,6,8,128]{4,3,2,1,0:T(8,128)(2,1)} collective-permute-done((bf16[4,3,6,8,128]{4,3,2,1,0:T(8,128)(2,1)S(1)}, bf16[4,3,6,8,128]{4,3,2,1,0:T(8,128)(2,1)}, u32[]{:S(2)}, u32[]{:S(2)}) %collective-permute-start.10) | collective-permute-done | bytes 147488 | tf_op jit(solution)/shard_map/cond/branch_0_fun/ppermute | solution.py:389
  167.7 1.0 fusion.2
  168.7 1.0 collective-permute-start.18
  169.7 6.4 %collective-permute-done.18.across_ref = bf16[144,8,128]{2,1,0:T(8,128)(2,1)S(1)} collective-permute-done((bf16[144,8,128]{2,1,0:T(8,128)(2,1)S(1)}, bf16[144,8,128]{2,1,0:T(8,128)(2,1)S(1)}, u32[]{:S(2)}, u32[]{:S(2)}) %collective-permute-start.18) | collective-permute-done | bytes 294944 | tf_op jit(solution)/shard_map/ppermute | solution.py:393
  176.1 2.2 %collective-permute-start.19 = (bf16[2,144,8,128]{3,2,1,0:T(8,128)(2,1)S(1)}, bf16[2,144,8,128]{3,2,1,0:T(8,128)(2,1)S(1)}, u32[]{:S(2)}, u32[]{:S(2)}) collective-permute-start(bf16[2,144,8,128]{3,2,1,0:T(8,128)(2,1)S(1)} %pad_maximum_fusion.8), channel_id=1, source_target_pairs={{0,1},{1,0},{2,3},{3,2},{4,5},{5,4},{6,7},{7,6},{8,9},{9,8},{10,11... | collective-permute-start | bytes 1769480 | tf_op jit(solution)/shard_map/ppermute | solution.py:393
  178.3 1.6 collective-permute-done.19.mate_ref
  180.0 0.8 copy-done.5
  180.8 9.9 %coarse_ff.1 = (f32[288,1024]{1,0:T(8,128)}, bf16[288,1024]{1,0:T(8,128)(2,1)}) custom-call(bf16[144,8,128]{2,1,0:T(8,128)(2,1)} %bitcast.49, bf16[144,8,128]{2,1,0:T(8,128)(2,1)} %copy-done.4, bf16[2,144,8,128]{3,2,1,0:T(8,128)(2,1)} %copy-done.5, f32[1,1024]{1,0:T(1,128)} %bitcast.63, bf16[4,512,1024]{2,1,0:T(8,128)(2,1)} %bitcast.51), custom_call_target="tpu_custom_call" | custom-call | tf_op jit(solution)/shard_map/coarse_ff/pallas_call | solution.py:324
  190.7 0.4 collective-permute-start.20
  191.1 1.8 collective-permute-done.20.mate_ref
  192.9 1.3 add_convert_fusion
  194.2 1.0 collective-permute-start.21
  195.2 7.3 %collective-permute-done.21.across_ref = bf16[144,1024]{1,0:T(8,128)(2,1)S(1)} collective-permute-done((bf16[144,1024]{1,0:T(8,128)(2,1)S(1)}, bf16[144,1024]{1,0:T(8,128)(2,1)S(1)}, u32[]{:S(2)}, u32[]{:S(2)}) %collective-permute-start.21) | collective-permute-done | bytes 294944 | tf_op jit(solution)/shard_map/ppermute | solution.py:393
  202.5 0.7 copy-done.10
  203.3 5.1 %blend.1 = (bf16[4,12,12,512]{3,2,1,0:T(8,128)(2,1)}, bf16[4,6,6,1024]{3,2,1,0:T(8,128)(2,1)}) custom-call(bf16[144,8,128]{2,1,0:T(8,128)(2,1)} %bitcast.50, f32[288,1024]{1,0:T(8,128)} %get-tuple-element.67.keep_ref, bf16[288,1024]{1,0:T(8,128)(2,1)} %copy-done.3, bf16[144,1024]{1,0:T(8,128)(2,1)} %copy-done.10, bf16[1024,2048]{1,0:T(8,128)(2,1)} %wu_ref.1, ...), custom_call_target="tpu_custom_call" | custom-call | tf_op jit(solution)/shard_map/blend/pallas_call | solution.py:367
  208.4 2.5 %copy.44 = bf16[4,12,12,512]{3,0,2,1:T(4,128)(2,1)} copy(bf16[4,12,12,512]{3,2,1,0:T(8,128)(2,1)} %get-tuple-element.80) | data formatting | bytes 1179648 | tf_op jit(solution)/shard_map/blend/pallas_call | solution.py:367
  210.8 0.9 copy.45
  (48 shorter events, 0.9 us)
Async XLA Ops:
  7.2 1.7 copy-start.8
  7.2 1.7 copy-start.11
  7.2 128.5 %all-gather.5.cloned.1.call-start = ((), (), s32[]{:S(2)}) async-start(), calls=%async_computation | async-start | bytes 13926400 | tf_op jit(solution)/shard_map/all_gather | solution.py:481
  8.8 1.1 copy-start.6
  8.9 1.4 copy-start.7
  9.9 168.5 %all-gather.7.cloned.1.call-start = ((), (), s32[]{:S(2)}) async-start(), calls=%async_computation.1 | async-start | bytes 5242880 | tf_op jit(solution)/shard_map/all_gather | solution.py:484
  10.2 1.3 copy-start.12
  10.2 9.7 %copy-start = (bf16[4,12,12,512]{3,0,2,1:T(4,128)(2,1)S(1)}, bf16[4,12,12,512]{3,0,2,1:T(4,128)(2,1)}, u32[]{:S(2)}) copy-start(bf16[4,12,12,512]{3,0,2,1:T(4,128)(2,1)} %param.35) | copy-start | bytes 1769476
  11.4 25.4 %copy-start.2 = (bf16[512,1536]{1,0:T(8,128)(2,1)S(1)}, bf16[512,1536]{1,0:T(8,128)(2,1)}, u32[]{:S(2)}) copy-start(bf16[512,1536]{1,0:T(8,128)(2,1)} %param.38) | copy-start | bytes 4718596
  20.1 16.7 %collective-permute-start.1 = (bf16[4,12,6,512]{3,2,1,0:T(8,128)(2,1)S(1)}, bf16[4,12,6,512]{3,2,1,0:T(8,128)(2,1)}, u32[]{:S(2)}, u32[]{:S(2)}) collective-permute-start(bf16[4,12,6,512]{3,2,1,0:T(8,128)(2,1)S(1)} %slice.49), channel_id=1, source_target_pairs={{1,0},{2,1},{3,2},{4,3},{5,4},{6,5},{7,6},{8,7},{9,8},{10,9},{11,1... | collective-permute-start | bytes 884744 | tf_op jit(solution)/shard_map/cond/branch_1_fun/ppermute | solution.py:389
  42.7 14.8 %collective-permute-start.12 = (bf16[4,3,18,512]{3,2,1,0:T(8,128)(2,1)S(1)}, bf16[4,3,18,512]{3,2,1,0:T(8,128)(2,1)}, u32[]{:S(2)}, u32[]{:S(2)}) collective-permute-start(bf16[4,3,18,512]{3,2,1,0:T(8,128)(2,1)S(1)} %pad_maximum_fusion), channel_id=1, source_target_pairs={{112,0},{0,16},{16,32},{32,48},{48,64},{64,80},{80,96},{96,112},{1... | collective-permute-start | bytes 663560 | tf_op jit(solution)/shard_map/cond/branch_0_fun/ppermute | solution.py:389
  69.3 5.5 %collective-permute-start.3 = (bf16[4,12,6,512]{3,2,1,0:T(8,128)(2,1)S(1)}, bf16[4,12,6,512]{3,2,1,0:T(8,128)(2,1)}, u32[]{:S(2)}, u32[]{:S(2)}) collective-permute-start(bf16[4,12,6,512]{3,2,1,0:T(8,128)(2,1)S(1)} %slice.55), channel_id=1, source_target_pairs={{15,0},{0,1},{1,2},{2,3},{3,4},{4,5},{5,6},{6,7},{7,8},{8,9},{9,10... | collective-permute-start | bytes 884744 | tf_op jit(solution)/shard_map/cond/branch_1_fun/ppermute | solution.py:389
  75.8 17.8 %collective-permute-start.14 = (bf16[4,3,18,512]{3,2,1,0:T(8,128)(2,1)S(1)}, bf16[4,3,18,512]{3,2,1,0:T(8,128)(2,1)}, u32[]{:S(2)}, u32[]{:S(2)}) collective-permute-start(bf16[4,3,18,512]{3,2,1,0:T(8,128)(2,1)S(1)} %pad_maximum_fusion.2), channel_id=1, source_target_pairs={{16,0},{32,16},{48,32},{64,48},{80,64},{96,80},{112,96},{0,112},{1... | collective-permute-start | bytes 663560 | tf_op jit(solution)/shard_map/cond/branch_0_fun/ppermute | solution.py:389
  106.0 8.4 %collective-permute-start.4 = (bf16[4,3,6,8,128]{4,3,2,1,0:T(8,128)(2,1)S(1)}, bf16[4,3,6,8,128]{4,3,2,1,0:T(8,128)(2,1)}, u32[]{:S(2)}, u32[]{:S(2)}) collective-permute-start(bf16[4,3,6,8,128]{4,3,2,1,0:T(8,128)(2,1)S(1)} %slice.60), channel_id=1, source_target_pairs={{112,0},{0,16},{16,32},{32,48},{48,64},{64,80},{80,96},{96,112},{1... | collective-permute-start | bytes 442376 | tf_op jit(solution)/shard_map/cond/branch_0_fun/ppermute | solution.py:389
  115.5 1.5 collective-permute-start.16
  117.0 18.0 %collective-permute-start.6 = (bf16[2,6,6,8,128]{4,3,2,1,0:T(8,128)(2,1)S(1)}, bf16[2,6,6,8,128]{4,3,2,1,0:T(8,128)(2,1)}, u32[]{:S(2)}, u32[]{:S(2)}) collective-permute-start(bf16[2,6,6,8,128]{4,3,2,1,0:T(8,128)(2,1)S(1)} %param.10), channel_id=1, source_target_pairs={{14,0},{15,1},{0,2},{1,3},{2,4},{3,5},{4,6},{5,7},{6,8},{7,9},{8,1... | collective-permute-start | bytes 442376 | tf_op jit(solution)/shard_map/cond/branch_0_fun/ppermute | solution.py:398
  148.2 8.7 %collective-permute-start.8 = (bf16[2,6,6,8,128]{4,3,2,1,0:T(8,128)(2,1)S(1)}, bf16[2,6,6,8,128]{4,3,2,1,0:T(8,128)(2,1)}, u32[]{:S(2)}, u32[]{:S(2)}) collective-permute-start(bf16[2,6,6,8,128]{4,3,2,1,0:T(8,128)(2,1)S(1)} %slice.62), channel_id=1, source_target_pairs={{2,0},{3,1},{4,2},{5,3},{6,4},{7,5},{8,6},{9,7},{10,8},{11,9},{12,... | collective-permute-start | bytes 442376 | tf_op jit(solution)/shard_map/cond/branch_0_fun/ppermute | solution.py:398
  158.0 2.9 %collective-permute-start.17 = (bf16[2,6,6,8,128]{4,3,2,1,0:T(8,128)(2,1)S(1)}, bf16[2,6,6,8,128]{4,3,2,1,0:T(8,128)(2,1)S(1)}, u32[]{:S(2)}, u32[]{:S(2)}) collective-permute-start(bf16[2,6,6,8,128]{4,3,2,1,0:T(8,128)(2,1)S(1)} %constant_dynamic-slice_fusion), channel_id=1, source_target_pairs={{0,1},{1,0},{2,3},{3,2},{4,5},{5,4},{6,7},{7,6},{8,9},{9,8},{10,11... | collective-permute-start | bytes 442376 | tf_op jit(solution)/shard_map/ppermute | solution.py:393
  161.0 6.8 %collective-permute-start.10 = (bf16[4,3,6,8,128]{4,3,2,1,0:T(8,128)(2,1)S(1)}, bf16[4,3,6,8,128]{4,3,2,1,0:T(8,128)(2,1)}, u32[]{:S(2)}, u32[]{:S(2)}) collective-permute-start(bf16[4,3,6,8,128]{4,3,2,1,0:T(8,128)(2,1)S(1)} %slice.64), channel_id=1, source_target_pairs={{16,0},{32,16},{48,32},{64,48},{80,64},{96,80},{112,96},{0,112},{1... | collective-permute-start | bytes 442376 | tf_op jit(solution)/shard_map/cond/branch_0_fun/ppermute | solution.py:389
  168.7 11.3 %copy-start.1 = (bf16[4,6,6,8,128]{4,3,2,1,0:T(8,128)(2,1)}, bf16[4,6,6,8,128]{4,3,2,1,0:T(8,128)(2,1)S(1)}, u32[]{:S(2)}) copy-start(bf16[4,6,6,8,128]{4,3,2,1,0:T(8,128)(2,1)S(1)} %fusion.2) | copy-start | bytes 884740
  168.7 7.4 %collective-permute-start.18 = (bf16[144,8,128]{2,1,0:T(8,128)(2,1)S(1)}, bf16[144,8,128]{2,1,0:T(8,128)(2,1)S(1)}, u32[]{:S(2)}, u32[]{:S(2)}) collective-permute-start(bf16[144,8,128]{2,1,0:T(8,128)(2,1)S(1)} %bitcast.47), channel_id=1, source_target_pairs={{0,8},{1,9},{2,10},{3,11},{4,12},{5,13},{6,14},{7,15},{8,0},{9,1},... | collective-permute-start | bytes 884744 | tf_op jit(solution)/shard_map/ppermute | solution.py:393
  176.1 3.9 %copy-start.4 = (bf16[144,8,128]{2,1,0:T(8,128)(2,1)}, bf16[144,8,128]{2,1,0:T(8,128)(2,1)S(1)}, u32[]{:S(2)}) copy-start(bf16[144,8,128]{2,1,0:T(8,128)(2,1)S(1)} %collective-permute-done.18.across_ref) | copy-start | bytes 884740
  176.1 3.8 %collective-permute-start.19 = (bf16[2,144,8,128]{3,2,1,0:T(8,128)(2,1)S(1)}, bf16[2,144,8,128]{3,2,1,0:T(8,128)(2,1)S(1)}, u32[]{:S(2)}, u32[]{:S(2)}) collective-permute-start(bf16[2,144,8,128]{3,2,1,0:T(8,128)(2,1)S(1)} %pad_maximum_fusion.8), channel_id=1, source_target_pairs={{0,1},{1,0},{2,3},{3,2},{4,5},{5,4},{6,7},{7,6},{8,9},{9,8},{10,11... | collective-permute-start | bytes 1769480 | tf_op jit(solution)/shard_map/ppermute | solution.py:393
  180.0 0.8 copy-start.5
  190.7 2.2 %collective-permute-start.20 = (bf16[288,1024]{1,0:T(8,128)(2,1)}, bf16[288,1024]{1,0:T(8,128)(2,1)S(1)}, u32[]{:S(2)}, u32[]{:S(2)}) collective-permute-start(bf16[288,1024]{1,0:T(8,128)(2,1)} %get-tuple-element.68), channel_id=1, source_target_pairs={{0,1},{1,0},{2,3},{3,2},{4,5},{5,4},{6,7},{7,6},{8,9},{9,8},{10,11... | collective-permute-start | bytes 1769480 | tf_op jit(solution)/shard_map/ppermute | solution.py:393
  192.9 9.7 %copy-start.3 = (bf16[288,1024]{1,0:T(8,128)(2,1)}, bf16[288,1024]{1,0:T(8,128)(2,1)S(1)}, u32[]{:S(2)}) copy-start(bf16[288,1024]{1,0:T(8,128)(2,1)S(1)} %collective-permute-done.20.mate_ref) | copy-start | bytes 1769476
  194.2 8.3 %collective-permute-start.21 = (bf16[144,1024]{1,0:T(8,128)(2,1)S(1)}, bf16[144,1024]{1,0:T(8,128)(2,1)S(1)}, u32[]{:S(2)}, u32[]{:S(2)}) collective-permute-start(bf16[144,1024]{1,0:T(8,128)(2,1)S(1)} %add_convert_fusion), channel_id=1, source_target_pairs={{0,8},{1,9},{2,10},{3,11},{4,12},{5,13},{6,14},{7,15},{8,0},{9,1},... | collective-permute-start | bytes 884744 | tf_op jit(solution)/shard_map/ppermute | solution.py:393
  202.5 0.7 copy-start.10
  208.4 2.5 %copy-start.9 = (bf16[4,6,6,1024]{3,2,1,0:T(8,128)(2,1)S(1)}, bf16[4,6,6,1024]{3,2,1,0:T(8,128)(2,1)}, u32[]{:S(2)}) copy-start(bf16[4,6,6,1024]{3,2,1,0:T(8,128)(2,1)} %get-tuple-element.81) | copy-start | bytes 884740
Sparse Core Ops, SparseCore 0:
  10.0 95.2 all-gather.4
  107.0 52.7 all-gather.6
